TPU v7x, 128 devices: a whole 4x4x4 slice. The times are simulated.
128 devices in a mesh: row: 8 (over z_lo, y), col: 16 (over x, z_hi, core).
Axes of the slice: x: 4, y: 4, z: 4 (z_hi: 2, z_lo: 2; z = z_hi * 2 + z_lo), core: 2. Of those that a mesh axis runs over, the one named last changes fastest.
Arguments:
- single: bfloat16 [2048, 384], P(('row', 'col')), may hold values from -6 to 6
- pair_input: bfloat16 [2048, 2048, 128], P('row', 'col'), may hold values from -6 to 6
- segment_lengths: int32 [8], replicated, may hold values from 1 to 512, 2048 in all
- single_gain: float32 [384], replicated, may hold values from 0.5 to 1.5
- w_left: bfloat16 [384, 32], replicated, may hold values from -0.3125 to 0.3125
- w_right: bfloat16 [384, 32], replicated, may hold values from -0.3125 to 0.3125
- w_outer: bfloat16 [1024, 128], replicated, may hold values from -0.1875 to 0.1875
- pair_gain: float32 [128], replicated, may hold values from 0.5 to 1.5
- w_gate: bfloat16 [128, 512], replicated, may hold values from -0.5 to 0.5
- w_up: bfloat16 [128, 512], replicated, may hold values from -0.5 to 0.5
- w_down: bfloat16 [512, 128], replicated, may hold values from -0.25 to 0.25
- bias_gain: float32 [128], replicated, may hold values from 0.5 to 1.5
- w_bias: bfloat16 [128, 16], replicated, may hold values from -8 to 8
- w_query: bfloat16 [384, 384], replicated, may hold values from -0.3125 to 0.3125
- w_key: bfloat16 [384, 384], replicated, may hold values from -0.3125 to 0.3125
- w_value: bfloat16 [384, 384], replicated, may hold values from -0.3125 to 0.3125
- w_gate_attn: bfloat16 [384, 384], replicated, may hold values from -0.3125 to 0.3125
- w_output: bfloat16 [384, 384], replicated, may hold values from -0.3125 to 0.3125
Outputs:
- single_out: bfloat16 [2048, 384], P(('row', 'col'))
- pair_out: bfloat16 [2048, 2048, 128], P('row', 'col')
Inputs may be any that keep to these rules, and one draw needn't show every extreme that they name: `segment_lengths`: the last entry is the number of padding tokens at the end of the window; the others are chain lengths.
All inputs are finite; a program needn't handle non-finite values.
Results may differ from a plain program's by a relative error of at most 0.0085.
The roundings to bfloat16 on the way count: a program that leaves them out, or rounds other values in their place, can miss the bound.
Values may be sent and summed in bfloat16 or wider, within the bound.
A program may use at most 128 MiB of HBM per device.

v0:
```python
import math

import jax
import jax.numpy as jnp
from jax import lax
from jax.sharding import PartitionSpec as P

EPSILON = 1e-05


def normalize(values, gain_vector):
    average = jnp.mean(values, -1, keepdims=True)
    centered = values - average
    variance = jnp.mean(centered * centered, -1, keepdims=True)
    return centered * lax.rsqrt(variance + EPSILON) * gain_vector


def matmul(left_side, right_side):
    return jnp.dot(left_side, right_side, preferred_element_type=jnp.float32)


def on_device(
    single,
    pair_input,
    segment_lengths,
    single_gain,
    w_left,
    w_right,
    w_outer,
    pair_gain,
    w_gate,
    w_up,
    w_down,
    bias_gain,
    w_bias,
    w_query,
    w_key,
    w_value,
    w_gate_attn,
    w_output,
):
    row_count = pair_input.shape[0]
    col_count = pair_input.shape[1]
    pair_width = pair_input.shape[2]
    own_count = single.shape[0]
    single_width = single.shape[1]
    head_count = w_bias.shape[1]
    head_dim = single_width // head_count
    outer_width = w_left.shape[1]
    row_devices = lax.axis_size("row")
    row_index = lax.axis_index("row")
    col_index = lax.axis_index("col")
    token_total = row_count * row_devices
    valid_limit = token_total - segment_lengths[segment_lengths.shape[0] - 1]
    row_start = row_index * row_count
    col_start = col_index * col_count

    def alive_mask(first_token, length):
        return (first_token + jnp.arange(length, dtype=jnp.int32) < valid_limit).astype(
            jnp.float32
        )[:, None]

    own_norm = normalize(single.astype(jnp.float32), single_gain).astype(jnp.bfloat16)
    gate_lin = matmul(own_norm, w_gate_attn)
    everything = lax.all_gather(single, ("row", "col"), axis=0, tiled=True)
    row_norm = normalize(
        lax.dynamic_slice_in_dim(everything, row_start, row_count, 0).astype(jnp.float32),
        single_gain,
    ).astype(jnp.bfloat16)
    col_norm = normalize(
        lax.dynamic_slice_in_dim(everything, col_start, col_count, 0).astype(jnp.float32),
        single_gain,
    ).astype(jnp.bfloat16)
    left_rows = (matmul(row_norm, w_left) * alive_mask(row_start, row_count)).astype(jnp.bfloat16)
    query_rows = matmul(row_norm, w_query).astype(jnp.bfloat16)
    right_cols = (matmul(col_norm, w_right) * alive_mask(col_start, col_count)).astype(jnp.bfloat16)
    key_cols = matmul(col_norm, w_key).astype(jnp.bfloat16)
    value_cols = matmul(col_norm, w_value).astype(jnp.bfloat16)
    outer_table = w_outer.reshape(outer_width, outer_width, pair_width)
    right_table = jnp.einsum(
        "jd,cdz->cjz", right_cols, outer_table, preferred_element_type=jnp.float32
    ).astype(jnp.bfloat16)
    right_table = right_table.reshape(outer_width, col_count * pair_width)
    keys_head = key_cols.reshape(col_count, head_count, head_dim)
    values_head = value_cols.reshape(col_count, head_count, head_dim)
    col_alive = col_start + jnp.arange(col_count, dtype=jnp.int32) < valid_limit
    score_scale = 1.0 / math.sqrt(head_dim)
    block_rows = math.gcd(row_count, 32)
    block_total = row_count // block_rows

    def one_block(offset):
        left_block = lax.dynamic_slice_in_dim(left_rows, offset, block_rows, 0)
        pair_block = lax.dynamic_slice_in_dim(pair_input, offset, block_rows, 0)
        middle = pair_block.astype(jnp.float32) + matmul(left_block, right_table).reshape(
            block_rows, col_count, pair_width
        )
        normed = (
            normalize(middle, pair_gain)
            .astype(jnp.bfloat16)
            .reshape(block_rows * col_count, pair_width)
        )
        hidden = (jax.nn.silu(matmul(normed, w_gate)) * matmul(normed, w_up)).astype(jnp.bfloat16)
        new_pair = (
            middle + matmul(hidden, w_down).reshape(block_rows, col_count, pair_width)
        ).astype(jnp.bfloat16)
        bias_input = (
            normalize(new_pair.astype(jnp.float32), bias_gain)
            .astype(jnp.bfloat16)
            .reshape(block_rows * col_count, pair_width)
        )
        pair_bias = matmul(bias_input, w_bias).reshape(block_rows, col_count, head_count)
        query_block = lax.dynamic_slice_in_dim(query_rows, offset, block_rows, 0).reshape(
            block_rows, head_count, head_dim
        )
        scores = (
            jnp.einsum("ihd,jhd->hij", query_block, keys_head, preferred_element_type=jnp.float32)
            * score_scale
        )
        scores = scores + jnp.transpose(pair_bias, (2, 0, 1))
        scores = jnp.where(col_alive[None, None, :], scores, -1e30)
        return (new_pair, scores)

    offsets = jnp.arange(block_total, dtype=jnp.int32) * block_rows
    new_pairs, scores = lax.map(one_block, offsets)
    pair_out = new_pairs.reshape(row_count, col_count, pair_width)
    local_peak = jnp.transpose(jnp.max(scores, -1), (0, 2, 1)).reshape(row_count, head_count)
    row_peak = lax.pmax(local_peak, "col")
    peak_blocks = jnp.transpose(row_peak.reshape(block_total, block_rows, head_count), (0, 2, 1))
    weights = jnp.exp(scores - peak_blocks[..., None])
    denominator = jnp.transpose(jnp.sum(weights, -1), (0, 2, 1)).reshape(row_count, head_count)
    numerator = jnp.einsum(
        "bhij,jhd->bihd",
        weights.astype(jnp.bfloat16),
        values_head,
        preferred_element_type=jnp.float32,
    )
    numerator = numerator.reshape(row_count, single_width)
    numerator, denominator = (
        lax.psum(numerator.astype(jnp.bfloat16), "col").astype(jnp.float32),
        lax.psum(denominator.astype(jnp.bfloat16), "col").astype(jnp.float32),
    )
    own_rows = col_index * own_count
    numerator = lax.dynamic_slice_in_dim(numerator, own_rows, own_count, 0)
    denominator = lax.dynamic_slice_in_dim(denominator, own_rows, own_count, 0)
    attended = (
        numerator.reshape(own_count, head_count, head_dim) / denominator[:, :, None]
    ).reshape(own_count, single_width)
    gated = (jax.nn.sigmoid(gate_lin) * attended).astype(jnp.bfloat16)
    single_out = (single.astype(jnp.float32) + matmul(gated, w_output)).astype(jnp.bfloat16)
    return (single_out, pair_out)


def solution(mesh):
    in_specs = (
        P(("row", "col"), None),
        P("row", "col", None),
        P(),
        P(),
        P(),
        P(),
        P(),
        P(),
        P(),
        P(),
        P(),
        P(),
        P(),
        P(),
        P(),
        P(),
        P(),
        P(),
    )
    out_specs = (P(("row", "col"), None), P("row", "col", None))
    return jax.shard_map(
        on_device, mesh=mesh, in_specs=in_specs, out_specs=out_specs, check_vma=False
    )
```

profile of v0, /device:TPU:1, one launch (start us, length us, event | category | flops | bytes accessed | tf_op | source)
XLA Modules:
  0.0 682.7 jit_solution(7673028879875781972)
XLA Ops:
  12.8 195.4 %all-gather.2.cloned.1.call-done = bf16[2048,384]{1,0:T(8,128)(2,1)} async-done(((bf16[16,384]{1,0:T(8,128)(2,1)}), bf16[2048,384]{1,0:T(8,128)(2,1)}) %all-gather.2.cloned.1.call-update) | async-done | bytes 1572880 | tf_op jit(solution)/shard_map/all_gather | solution.py:65
  221.4 249.4 %while.13 = (s32[]{:T(128)}, bf16[8,32,128,128]{3,2,1,0:T(8,128)(2,1)}, f32[8,16,32,128]{3,2,1,0:T(8,128)}, s32[8]{0:T(128)S(1)}, bf16[256,128,128]{2,1,0:T(8,12...) while((s32[]{:T(128)}, ...), condition=%wide.region_11.12_spmd.clone, body=%wide.region_6.11_spmd.clone.sunk | while | flops 1692082432 | bytes 61893216 | solution.py:124
  233.1 4.5 fusion.118
  237.5 8.0 %fusion.119 = f32[4096,128]{1,0:T(8,128)} fusion(bf16[512,128]{1,0:T(8,128)(2,1)} %get-tuple-element.388, f32[4096,512]{1,0:T(8,128)} %fusion.118, bf16[4096,128]{1,0:T(8,128)(2,1)S(1)} %bitcast.113, bf16[128,512]{1,0:T(8,128)(2,1)} %get-tuple-element.387), kind=kOutput, calls=%fused_computation.13.clone.1 | convolution fusion | flops 1086324736 | bytes 11796480 | tf_op jit(solution)/shard_map/while/body/eval_jaxpr/dot_general | solution.py:19
  245.6 2.5 convert_reduce_fusion.5
  264.2 4.5 fusion.118
  268.7 8.0 %fusion.119 = f32[4096,128]{1,0:T(8,128)} fusion(bf16[512,128]{1,0:T(8,128)(2,1)} %get-tuple-element.388, f32[4096,512]{1,0:T(8,128)} %fusion.118, bf16[4096,128]{1,0:T(8,128)(2,1)S(1)} %bitcast.113, bf16[128,512]{1,0:T(8,128)(2,1)} %get-tuple-element.387), kind=kOutput, calls=%fused_computation.13.clone.1 | convolution fusion | flops 1086324736 | bytes 11796480 | tf_op jit(solution)/shard_map/while/body/eval_jaxpr/dot_general | solution.py:19
  276.7 2.5 convert_reduce_fusion.5
  295.4 4.5 fusion.118
  299.8 8.0 %fusion.119 = f32[4096,128]{1,0:T(8,128)} fusion(bf16[512,128]{1,0:T(8,128)(2,1)} %get-tuple-element.388, f32[4096,512]{1,0:T(8,128)} %fusion.118, bf16[4096,128]{1,0:T(8,128)(2,1)S(1)} %bitcast.113, bf16[128,512]{1,0:T(8,128)(2,1)} %get-tuple-element.387), kind=kOutput, calls=%fused_computation.13.clone.1 | convolution fusion | flops 1086324736 | bytes 11796480 | tf_op jit(solution)/shard_map/while/body/eval_jaxpr/dot_general | solution.py:19
  326.5 4.5 fusion.118
  331.0 8.0 %fusion.119 = f32[4096,128]{1,0:T(8,128)} fusion(bf16[512,128]{1,0:T(8,128)(2,1)} %get-tuple-element.388, f32[4096,512]{1,0:T(8,128)} %fusion.118, bf16[4096,128]{1,0:T(8,128)(2,1)S(1)} %bitcast.113, bf16[128,512]{1,0:T(8,128)(2,1)} %get-tuple-element.387), kind=kOutput, calls=%fused_computation.13.clone.1 | convolution fusion | flops 1086324736 | bytes 11796480 | tf_op jit(solution)/shard_map/while/body/eval_jaxpr/dot_general | solution.py:19
  339.0 2.5 convert_reduce_fusion.5
  357.7 4.5 fusion.118
  362.1 8.0 %fusion.119 = f32[4096,128]{1,0:T(8,128)} fusion(bf16[512,128]{1,0:T(8,128)(2,1)} %get-tuple-element.388, f32[4096,512]{1,0:T(8,128)} %fusion.118, bf16[4096,128]{1,0:T(8,128)(2,1)S(1)} %bitcast.113, bf16[128,512]{1,0:T(8,128)(2,1)} %get-tuple-element.387), kind=kOutput, calls=%fused_computation.13.clone.1 | convolution fusion | flops 1086324736 | bytes 11796480 | tf_op jit(solution)/shard_map/while/body/eval_jaxpr/dot_general | solution.py:19
  388.8 4.5 fusion.118
  393.3 8.0 %fusion.119 = f32[4096,128]{1,0:T(8,128)} fusion(bf16[512,128]{1,0:T(8,128)(2,1)} %get-tuple-element.388, f32[4096,512]{1,0:T(8,128)} %fusion.118, bf16[4096,128]{1,0:T(8,128)(2,1)S(1)} %bitcast.113, bf16[128,512]{1,0:T(8,128)(2,1)} %get-tuple-element.387), kind=kOutput, calls=%fused_computation.13.clone.1 | convolution fusion | flops 1086324736 | bytes 11796480 | tf_op jit(solution)/shard_map/while/body/eval_jaxpr/dot_general | solution.py:19
  420.0 4.5 fusion.118
  424.4 8.0 %fusion.119 = f32[4096,128]{1,0:T(8,128)} fusion(bf16[512,128]{1,0:T(8,128)(2,1)} %get-tuple-element.388, f32[4096,512]{1,0:T(8,128)} %fusion.118, bf16[4096,128]{1,0:T(8,128)(2,1)S(1)} %bitcast.113, bf16[128,512]{1,0:T(8,128)(2,1)} %get-tuple-element.387), kind=kOutput, calls=%fused_computation.13.clone.1 | convolution fusion | flops 1086324736 | bytes 11796480 | tf_op jit(solution)/shard_map/while/body/eval_jaxpr/dot_general | solution.py:19
  451.1 4.5 fusion.118
  455.6 8.0 %fusion.119 = f32[4096,128]{1,0:T(8,128)} fusion(bf16[512,128]{1,0:T(8,128)(2,1)} %get-tuple-element.388, f32[4096,512]{1,0:T(8,128)} %fusion.118, bf16[4096,128]{1,0:T(8,128)(2,1)S(1)} %bitcast.113, bf16[128,512]{1,0:T(8,128)(2,1)} %get-tuple-element.387), kind=kOutput, calls=%fused_computation.13.clone.1 | convolution fusion | flops 1086324736 | bytes 11796480 | tf_op jit(solution)/shard_map/while/body/eval_jaxpr/dot_general | solution.py:19
  473.2 62.1 %pmax.7 = f32[8,16,32]{2,1,0:T(8,128)S(1)} all-reduce(f32[8,16,32]{2,1,0:T(8,128)S(1)} %reduce_max.9), channel_id=1, replica_groups=mesh['row'=8,'col'=16] {'col'}, use_global_device_ids=true, to_apply=%region_13.14 | all-reduce | flops 4096 | bytes 32768 | tf_op jit(solution)/shard_map/pmax | solution.py:127
  541.2 39.0 %psum.15 = bf16[256,16]{0,1:T(8,128)(2,1)S(1)} all-reduce(bf16[256,16]{0,1:T(8,128)(2,1)S(1)} %convert_element_type.127), channel_id=1, replica_groups=mesh['row'=8,'col'=16] {'col'}, use_global_device_ids=true, to_apply=%region_16.17 | all-reduce | flops 4096 | bytes 16384 | tf_op jit(solution)/shard_map/psum | solution.py:140
  580.6 93.6 %all-reduce.2.cloned.1.call-done = bf16[256,384]{1,0:T(8,128)(2,1)} async-done(((bf16[256,384]{1,0:T(8,128)(2,1)}), bf16[256,384]{1,0:T(8,128)(2,1)}) %all-reduce.2.cloned.1.call-update) | async-done | bytes 196624 | tf_op jit(solution)/shard_map/psum | solution.py:139
  (401 shorter events, 152.1 us)
Async XLA Ops:
  7.2 211.8 %copy-start = (bf16[384,384]{1,0:T(8,128)(2,1)S(1)}, bf16[384,384]{1,0:T(8,128)(2,1)}, u32[]{:S(2)}) copy-start(bf16[384,384]{1,0:T(8,128)(2,1)} %param.33) | copy-start | bytes 884740
  7.2 209.5 %copy-start.9 = (bf16[1024,128]{1,0:T(8,128)(2,1)S(1)}, bf16[1024,128]{1,0:T(8,128)(2,1)}, u32[]{:S(2)}) copy-start(bf16[1024,128]{1,0:T(8,128)(2,1)} %param.26) | copy-start | bytes 786436
  7.2 201.1 %all-gather.2.cloned.1.call-start = ((), (), s32[]{:S(2)}) async-start(), calls=%async_computation | async-start | bytes 1585152 | tf_op jit(solution)/shard_map/all_gather | solution.py:65
  7.9 666.2 %all-reduce.2.cloned.1.call-start = ((), (), s32[]{:S(2)}) async-start(), calls=%async_computation.1 | async-start | bytes 393216 | tf_op jit(solution)/shard_map/psum | solution.py:139
  214.6 4.4 copy-start.15
  245.6 3.9 copy-start.22
  276.7 3.9 copy-start.21
  276.7 3.9 copy-start.22
  307.8 3.9 copy-start.21
  307.8 3.9 copy-start.22
  339.0 3.9 copy-start.22
  370.2 3.9 copy-start.22
  401.3 3.9 copy-start.21
  401.3 3.9 copy-start.22
  432.4 3.9 copy-start.21
  432.4 3.9 copy-start.22
  463.6 3.9 copy-start.22
  470.8 64.5 %copy-start.3 = (f32[8,16,32,128]{3,2,1,0:T(8,128)S(1)}, f32[8,16,32,128]{3,2,1,0:T(8,128)}, u32[]{:S(2)}) copy-start(f32[8,16,32,128]{3,2,1,0:T(8,128)} %get-tuple-element.85) | copy-start | bytes 6291460
  473.2 63.4 %copy-start.6 = (bf16[128,384]{0,1:T(8,128)(2,1)S(1)}, bf16[128,384]{0,1:T(8,128)(2,1)}, u32[]{:S(2)}) copy-start(bf16[128,384]{0,1:T(8,128)(2,1)} %copy.42) | copy-start | bytes 294916
  538.1 136.0 %copy-start.7 = (bf16[384,384]{1,0:T(8,128)(2,1)S(1)}, bf16[384,384]{1,0:T(8,128)(2,1)}, u32[]{:S(2)}) copy-start(bf16[384,384]{1,0:T(8,128)(2,1)} %param.37) | copy-start | bytes 884740
  538.1 136.0 %copy-start.8 = (bf16[384,384]{1,0:T(8,128)(2,1)S(1)}, bf16[384,384]{1,0:T(8,128)(2,1)}, u32[]{:S(2)}) copy-start(bf16[384,384]{1,0:T(8,128)(2,1)} %param.36) | copy-start | bytes 884740
  538.2 136.0 %copy-start.10 = (bf16[16,384]{1,0:T(8,128)(2,1)S(1)}, bf16[16,384]{1,0:T(8,128)(2,1)}, u32[]{:S(2)}) copy-start(bf16[16,384]{1,0:T(8,128)(2,1)} %param.20) | copy-start | bytes 36868
  538.2 136.0 %copy-start.16 = (f32[384]{0:T(512)S(1)}, f32[384]{0:T(512)}, u32[]{:S(2)}) copy-start(f32[384]{0:T(512)} %param.23) | copy-start | bytes 4612
  538.2 136.0 %copy-start.18 = (f32[16]{0:T(128)S(1)}, f32[16]{0:T(128)}, u32[]{:S(2)}) copy-start(f32[16]{0:T(128)} %copy-done.17) | copy-start | bytes 196
  (87 other events, 268.1 us)
Sparse Core Ops, SparseCore 0:
  9.7 198.4 all-gather.1
  541.1 132.9 all-reduce.1
where the time goes:
time: 685 us; the launch traced here: 683 us
  waiting for transfers between devices  290 us (42%)
  matrix products  132 us (19%)
  other arithmetic  101 us (15%)
  blocking collectives  101 us (15%)
  local copies, waits for them, and re-layouts  26.2 us (4%)
  loops' own time  18.1 us (3%)
  between operations  15 us (2%)
    all_gather x1, waiting for transfers between devices, on_device(): everything = lax.all_gather(single, ('row', 'col'), axis=0, tiled=True)  195 us
    dot_general x37, matrix products, matmul(): return jnp.dot(left_side, right_side, preferred_element_type=jnp.float32)  121 us
    psum x1, waiting for transfers between devices, on_device(): lax.psum(numerator.astype(jnp.bfloat16), 'col').astype(jnp.float32)  93.6 us
    pmax x1, blocking collectives, on_device(): row_peak = lax.pmax(local_peak, 'col')  62.1 us
    reduce_sum x19, other arithmetic, normalize(): average = jnp.mean(values, -1, keepdims=True)  39.9 us
    psum x1, blocking collectives, on_device(): lax.psum(denominator.astype(jnp.bfloat16), 'col').astype(jnp.float32)  39 us
    reduce_sum x19, other arithmetic, normalize(): variance = jnp.mean(centered * centered, -1, keepdims=True)  33.2 us
    convert_element_type x8, other arithmetic, one_block(): normed = normalize(middle, pair_gain).astype(jnp.bfloat16).reshape(block_...  19 us
  transfers between devices with their start and end apart: 2, of which 2 were waited for; matrix products, arithmetic and copies ran while one was open for 1% of the time, Pallas kernels for 0%

commit v1 on v0

v1 whole, which is shorter than its diff:
```python
import functools
import math

import jax
import jax.numpy as jnp
from jax import lax
from jax.experimental import pallas as pl
from jax.experimental.pallas import tpu as pltpu
from jax.sharding import PartitionSpec as P

EPSILON = 1e-05
MESH = pl.DeviceIdType.MESH
BF16 = jnp.bfloat16
F32 = jnp.float32
VMEM_SPEC = pl.BlockSpec(memory_space=pltpu.VMEM)
CHUNK = 4
BLOCK = 16


def normalize(values, gain_vector):
    average = jnp.mean(values, -1, keepdims=True)
    centered = values - average
    variance = jnp.mean(centered * centered, -1, keepdims=True)
    return centered * lax.rsqrt(variance + EPSILON) * gain_vector


def matmul(left_side, right_side):
    return jnp.dot(left_side, right_side, preferred_element_type=F32)


def matmul_nt(left_side, right_side):
    return lax.dot_general(
        left_side, right_side, (((1,), (1,)), ((), ())), preferred_element_type=F32
    )


def gather_kernel(
    rows, cols, per_block, single_ref, row_ref, col_ref, send_row, send_col, recv_row, recv_col
):
    own = single_ref.shape[0]
    row, col = lax.axis_index("row"), lax.axis_index("col")
    linear = row * cols + col
    target_col = linear // per_block
    slot = linear % per_block
    is_own = target_col == col
    first_source = col * per_block

    barrier = pltpu.get_barrier_semaphore()
    for step in range(1, cols):
        pl.semaphore_signal(
            barrier, inc=1, device_id=(row, lax.rem(col + step, cols)), device_id_type=MESH
        )
    for step in range(per_block):
        source = first_source + step
        source_row, source_col = source // cols, source % cols

        @pl.when(source != linear)
        def _():
            pl.semaphore_signal(
                barrier, inc=1, device_id=(source_row, source_col), device_id_type=MESH
            )

    pl.semaphore_wait(barrier, cols - 1 + rows - is_own.astype(jnp.int32))

    own_rows = pl.ds(pl.multiple_of(col * own, own), own)
    own_cols = pl.ds(pl.multiple_of(slot * own, own), own)

    def row_copy(step):
        return pltpu.make_async_remote_copy(
            src_ref=single_ref,
            dst_ref=row_ref.at[own_rows],
            send_sem=send_row.at[step],
            recv_sem=recv_row.at[col],
            device_id=(row, lax.rem(col + step, cols)),
            device_id_type=MESH,
        )

    def col_copy(step):
        return pltpu.make_async_remote_copy(
            src_ref=single_ref,
            dst_ref=col_ref.at[own_cols],
            send_sem=send_col.at[step],
            recv_sem=recv_col.at[slot],
            device_id=(lax.rem(row + step, rows), target_col),
            device_id_type=MESH,
        )

    local_row = pltpu.make_async_copy(single_ref, row_ref.at[own_rows], recv_row.at[col])
    local_col = pltpu.make_async_copy(single_ref, col_ref.at[own_cols], recv_col.at[slot])
    for step in range(1, rows):
        col_copy(step).start()

    @pl.when(jnp.logical_not(is_own))
    def _():
        col_copy(0).start()

    for step in range(1, cols):
        row_copy(step).start()
    local_row.start()

    @pl.when(is_own)
    def _():
        local_col.start()

    for sender in range(cols):
        block = row_ref.at[pl.ds(sender * own, own)]
        pltpu.make_async_copy(block, block, recv_row.at[sender]).wait()
    for sender in range(per_block):
        block = col_ref.at[pl.ds(sender * own, own)]
        pltpu.make_async_copy(block, block, recv_col.at[sender]).wait()
    for step in range(1, cols):
        row_copy(step).wait_send()
    for step in range(1, rows):
        col_copy(step).wait_send()

    @pl.when(jnp.logical_not(is_own))
    def _():
        col_copy(0).wait_send()


def gather(single, rows, cols, row_count, col_count):
    own, width = single.shape
    per_block = col_count // own
    return pl.pallas_call(
        functools.partial(gather_kernel, rows, cols, per_block),
        out_shape=(
            jax.ShapeDtypeStruct((row_count, width), single.dtype),
            jax.ShapeDtypeStruct((col_count, width), single.dtype),
        ),
        in_specs=[VMEM_SPEC],
        out_specs=(VMEM_SPEC, VMEM_SPEC),
        scratch_shapes=[
            pltpu.SemaphoreType.DMA((cols,)),
            pltpu.SemaphoreType.DMA((rows,)),
            pltpu.SemaphoreType.DMA((cols,)),
            pltpu.SemaphoreType.DMA((per_block,)),
        ],
        compiler_params=pltpu.CompilerParams(collective_id=0, has_side_effects=True),
        name="gather_tokens",
    )(single)


def main_kernel(
    head_count,
    row_devices,
    seg_ref,
    row_ref,
    col_ref,
    sgain_ref,
    wl_ref,
    wr_ref,
    wo_ref,
    pgain_ref,
    wg_ref,
    wu_ref,
    wd_ref,
    bgain_ref,
    wb_ref,
    wq_ref,
    wk_ref,
    wv_ref,
    pair_ref,
    out_ref,
    num_ref,
    stat_ref,
    wo_scr,
    t_scr,
    right_scr,
    q_scr,
    k_scr,
    v_scr,
    wgu_scr,
    live_scr,
    bias_scr,
):
    step = pl.program_id(0)
    row_count, width = row_ref.shape
    col_count = col_ref.shape[0]
    outer = wl_ref.shape[0]
    pair_width = wb_ref.shape[1]
    head_dim = width // head_count
    hid = wg_ref.shape[1]
    limit = row_count * row_devices - seg_ref[seg_ref.shape[0] - 1]

    @pl.when(step == 0)
    def _():
        row_start = lax.axis_index("row") * row_count
        col_start = lax.axis_index("col") * col_count
        row_norm = normalize(row_ref[...].astype(F32), sgain_ref[...]).astype(BF16)
        col_norm = normalize(col_ref[...].astype(F32), sgain_ref[...]).astype(BF16)
        row_tokens = row_start + lax.broadcasted_iota(jnp.int32, (row_count, outer), 0)
        col_tokens = col_start + lax.broadcasted_iota(jnp.int32, (col_count, outer), 0)
        left = jnp.where(row_tokens < limit, matmul_nt(row_norm, wl_ref[...]), 0.0).astype(BF16)
        right = jnp.where(col_tokens < limit, matmul_nt(col_norm, wr_ref[...]), 0.0).astype(BF16)
        right_scr[...] = right
        q_scr[...] = matmul(row_norm, wq_ref[...]).astype(BF16)
        k_scr[...] = matmul(col_norm, wk_ref[...]).astype(BF16)
        v_scr[...] = matmul(col_norm, wv_ref[...]).astype(BF16)
        wgu_scr[:, :hid] = (wg_ref[...].astype(F32) * 0.5).astype(BF16)
        wgu_scr[:, hid:] = wu_ref[...]
        keys = col_start + lax.broadcasted_iota(jnp.int32, (8, col_count), 1)
        live_scr[...] = (keys < limit).astype(F32)
        wo_scr[...] = wo_ref[...].astype(F32)

        def table(pair, carry):
            d = pair * 2
            w0 = wo_scr[pl.ds(d, outer, stride=outer), :]
            w1 = wo_scr[pl.ds(d + 1, outer, stride=outer), :]
            both = matmul(left, jnp.concatenate([w0, w1], axis=1).astype(BF16))
            t_scr[pl.ds(d, row_count, stride=outer), :] = both[:, :pair_width]
            t_scr[pl.ds(d + 1, row_count, stride=outer), :] = both[:, pair_width:]
            return carry

        lax.fori_loop(0, outer // 2, table, 0)

    pgain = pgain_ref[...]
    bgain = bgain_ref[...]

    def chunk(index, carry):
        for half in range(CHUNK // 2):
            first = index * CHUNK + half * 2
            base = pl.multiple_of((step * BLOCK + first) * outer, 2 * outer)
            t_pair = t_scr[pl.ds(base, 2 * outer), :]
            t_cat = jnp.concatenate([t_pair[:outer], t_pair[outer:]], axis=1).astype(BF16)
            update = matmul(right_scr[...], t_cat)
            middle = jnp.concatenate(
                [
                    pair_ref[first].astype(F32) + update[:, :pair_width],
                    pair_ref[first + 1].astype(F32) + update[:, pair_width:],
                ],
                axis=0,
            )
            normed = normalize(middle, pgain).astype(BF16)
            both = matmul(normed, wgu_scr[...])
            half_gate, up = both[:, :hid], both[:, hid:]
            hidden = ((half_gate * jnp.tanh(half_gate) + half_gate) * up).astype(BF16)
            new_pair = (middle + matmul(hidden, wd_ref[...])).astype(BF16)
            out_ref[first] = new_pair[:col_count]
            out_ref[first + 1] = new_pair[col_count:]
            bias_input = normalize(new_pair.astype(F32), bgain).astype(BF16)
            bias = matmul_nt(wb_ref[...], bias_input)
            at = pl.multiple_of(first * head_count, 2 * head_count)
            bias_scr[pl.ds(at, 2 * head_count), :] = jnp.concatenate(
                [bias[:, :col_count], bias[:, col_count:]], axis=0
            )
        return carry

    lax.fori_loop(0, BLOCK // CHUNK, chunk, 0)

    pairs = BLOCK * head_count
    query = q_scr[pl.ds(pl.multiple_of(step * BLOCK, BLOCK), BLOCK), :].astype(F32)
    head_of = lax.broadcasted_iota(jnp.int32, (BLOCK, head_count, width), 2) // head_dim
    own_head = head_of == lax.broadcasted_iota(jnp.int32, (BLOCK, head_count, width), 1)
    spread = jnp.where(own_head, query[:, None, :], 0.0).reshape(pairs, width).astype(BF16)
    scores = matmul_nt(spread, k_scr[...]) * (1.0 / math.sqrt(head_dim)) + bias_scr[...]
    scores = jnp.where(live_scr[0:1, :] > 0.0, scores, -1e30)
    peak = jnp.max(scores, -1, keepdims=True)
    weights = jnp.exp(scores - peak)
    total = jnp.sum(weights, -1, keepdims=True)
    full = matmul(weights.astype(BF16), v_scr[...]).reshape(BLOCK, head_count, width)
    num_ref[...] = jnp.sum(jnp.where(own_head, full, 0.0), axis=1).astype(BF16)
    lane = lax.broadcasted_iota(jnp.int32, (BLOCK, head_count, 128), 2)
    head = lax.broadcasted_iota(jnp.int32, (BLOCK, head_count, 128), 1)
    peak_b = jnp.broadcast_to(peak, (pairs, 128)).reshape(BLOCK, head_count, 128)
    total_b = jnp.broadcast_to(total, (pairs, 128)).reshape(BLOCK, head_count, 128)
    stats = jnp.where(lane == head, peak_b, jnp.where(lane == head + head_count, total_b, 0.0))
    stat_ref[...] = jnp.sum(stats, axis=1)


def main(head_count, row_devices, seg, row_tokens, col_tokens, weights, pair_input):
    row_count, col_count, pair_width = pair_input.shape
    width = row_tokens.shape[1]
    outer = weights[1].shape[0]
    hid = weights[5].shape[1]

    def whole(array):
        return pl.BlockSpec(array.shape, lambda i: (0,) * array.ndim, pipeline_mode=pl.Buffered(1))

    pair_spec = pl.BlockSpec((BLOCK, col_count, pair_width), lambda i: (i, 0, 0))
    return pl.pallas_call(
        functools.partial(main_kernel, head_count, row_devices),
        grid=(row_count // BLOCK,),
        out_shape=(
            jax.ShapeDtypeStruct(pair_input.shape, BF16),
            jax.ShapeDtypeStruct((row_count, width), BF16),
            jax.ShapeDtypeStruct((row_count, 128), F32),
        ),
        in_specs=[
            pl.BlockSpec(memory_space=pltpu.SMEM),
            whole(row_tokens),
            whole(col_tokens),
            *[whole(w) for w in weights],
            pair_spec,
        ],
        out_specs=(
            pair_spec,
            pl.BlockSpec((BLOCK, width), lambda i: (i, 0)),
            pl.BlockSpec((BLOCK, 128), lambda i: (i, 0)),
        ),
        scratch_shapes=[
            pltpu.VMEM((outer * outer, pair_width), F32),
            pltpu.VMEM((row_count * outer, pair_width), F32),
            pltpu.VMEM((col_count, outer), BF16),
            pltpu.VMEM((row_count, width), BF16),
            pltpu.VMEM((col_count, width), BF16),
            pltpu.VMEM((col_count, width), BF16),
            pltpu.VMEM((pair_width, 2 * hid), BF16),
            pltpu.VMEM((8, col_count), F32),
            pltpu.VMEM((BLOCK * head_count, col_count), F32),
        ],
        compiler_params=pltpu.CompilerParams(
            dimension_semantics=("arbitrary",), vmem_limit_bytes=56 << 20
        ),
        name="pair_main",
    )(seg, row_tokens, col_tokens, *weights, pair_input)


def combine_kernel(
    cols,
    head_count,
    single_ref,
    sgain_ref,
    wga_ref,
    wo_ref,
    num_ref,
    stat_ref,
    out_ref,
    nums,
    stats,
    send_num,
    send_stat,
    recv_num,
    recv_stat,
):
    own, width = single_ref.shape
    head_dim = width // head_count
    row, col = lax.axis_index("row"), lax.axis_index("col")

    barrier = pltpu.get_barrier_semaphore()
    for step in range(1, cols):
        pl.semaphore_signal(
            barrier, inc=1, device_id=(row, lax.rem(col + step, cols)), device_id_type=MESH
        )
    single = single_ref[...].astype(F32)
    gate = matmul(normalize(single, sgain_ref[...]).astype(BF16), wga_ref[...])
    pl.semaphore_wait(barrier, cols - 1)

    def copies(step):
        peer = lax.rem(col + step, cols)
        block = pl.ds(pl.multiple_of(peer * own, own), own)
        return (
            pltpu.make_async_remote_copy(
                src_ref=num_ref.at[block],
                dst_ref=nums.at[col],
                send_sem=send_num.at[step],
                recv_sem=recv_num.at[col],
                device_id=(row, peer),
                device_id_type=MESH,
            ),
            pltpu.make_async_remote_copy(
                src_ref=stat_ref.at[block],
                dst_ref=stats.at[col],
                send_sem=send_stat.at[step],
                recv_sem=recv_stat.at[col],
                device_id=(row, peer),
                device_id_type=MESH,
            ),
        )

    for step in range(1, cols):
        for copy in copies(step):
            copy.start()
    block = pl.ds(pl.multiple_of(col * own, own), own)
    pltpu.make_async_copy(num_ref.at[block], nums.at[col], recv_num.at[col]).start()
    pltpu.make_async_copy(stat_ref.at[block], stats.at[col], recv_stat.at[col]).start()
    for sender in range(cols):
        pltpu.make_async_copy(nums.at[sender], nums.at[sender], recv_num.at[sender]).wait()
        pltpu.make_async_copy(stats.at[sender], stats.at[sender], recv_stat.at[sender]).wait()

    part = stats[...]
    top = jnp.max(part, axis=0)
    scale = jnp.exp(part - top[None])
    total = jnp.sum(scale * pltpu.roll(part, 128 - head_count, 2), axis=0)
    lane = lax.broadcasted_iota(jnp.int32, (128, width), 0)
    spread = (lane == lax.broadcasted_iota(jnp.int32, (128, width), 1) // head_dim).astype(F32)
    head_lane = lax.broadcasted_iota(jnp.int32, (own, 128), 1) < head_count
    share = jnp.where(head_lane[None], scale / total[None], 0.0).reshape(cols * own, 128)
    wide = jnp.dot(
        share, spread, precision=lax.Precision.HIGHEST, preferred_element_type=F32
    ).reshape(cols, own, width)
    attended = jnp.sum(wide * nums[...].astype(F32), axis=0)
    gated = (jax.nn.sigmoid(gate) * attended).astype(BF16)
    out_ref[...] = (single + matmul(gated, wo_ref[...])).astype(BF16)
    for step in range(1, cols):
        for copy in copies(step):
            copy.wait_send()


def combine(cols, head_count, single, single_gain, w_gate_attn, w_output, num, stat):
    own, width = single.shape
    return pl.pallas_call(
        functools.partial(combine_kernel, cols, head_count),
        out_shape=jax.ShapeDtypeStruct(single.shape, BF16),
        in_specs=[VMEM_SPEC] * 6,
        out_specs=VMEM_SPEC,
        scratch_shapes=[
            pltpu.VMEM((cols, own, width), BF16),
            pltpu.VMEM((cols, own, 128), F32),
            pltpu.SemaphoreType.DMA((cols,)),
            pltpu.SemaphoreType.DMA((cols,)),
            pltpu.SemaphoreType.DMA((cols,)),
            pltpu.SemaphoreType.DMA((cols,)),
        ],
        compiler_params=pltpu.CompilerParams(collective_id=1, has_side_effects=True),
        name="combine_parts",
    )(single, single_gain, w_gate_attn, w_output, num, stat)


def on_device(
    rows,
    cols,
    single,
    pair_input,
    segment_lengths,
    single_gain,
    w_left,
    w_right,
    w_outer,
    pair_gain,
    w_gate,
    w_up,
    w_down,
    bias_gain,
    w_bias,
    w_query,
    w_key,
    w_value,
    w_gate_attn,
    w_output,
):
    row_count, col_count, _ = pair_input.shape
    head_count = w_bias.shape[1]
    row_tokens, col_tokens = gather(single, rows, cols, row_count, col_count)
    weights = (
        single_gain[None, :],
        w_left.T,
        w_right.T,
        w_outer,
        pair_gain[None, :],
        w_gate,
        w_up,
        w_down,
        bias_gain[None, :],
        w_bias.T,
        w_query,
        w_key,
        w_value,
    )
    pair_out, num, stat = main(
        head_count, rows, segment_lengths, row_tokens, col_tokens, weights, pair_input
    )
    single_out = combine(
        cols, head_count, single, single_gain[None, :], w_gate_attn, w_output, num, stat
    )
    return (single_out, pair_out)


def solution(mesh):
    rows, cols = mesh.shape["row"], mesh.shape["col"]
    in_specs = (P(("row", "col"), None), P("row", "col", None), *([P()] * 16))
    out_specs = (P(("row", "col"), None), P("row", "col", None))
    return jax.shard_map(
        functools.partial(on_device, rows, cols),
        mesh=mesh,
        in_specs=in_specs,
        out_specs=out_specs,
        check_vma=False,
    )
```

time: 685 us -> 177 us (0.26)
  waiting for transfers between devices: 290 us -> 0 us
  Pallas kernels: 0 us -> 173 us
  matrix products: 132 us -> 0 us
  other arithmetic: 101 us -> 0 us
  blocking collectives: 101 us -> 0 us
  local copies, waits for them, and re-layouts: 26.2 us -> 2.55 us
  loops' own time: 18.1 us -> 0 us
  between operations: 15 us -> 0.65 us
    all_gather x1 -> x0, waiting for transfers between devices: 195 us -> none  [on_device(): everything = lax.all_gather(single, ('row', 'col'), axis=0, tiled=True)]
    pallas_call x0 -> x3, Pallas kernels: none -> 173 us  [the longest x1 141 us: main(): pl.pallas_call(functools.partial(main_kernel, head_count, row_devices), g...]
    dot_general x47 -> x0, matrix products: 132 us -> none  [the longest x37 121 us: matmul(): return jnp.dot(left_side, right_side, preferred_element_type=jnp.float32)]
    psum x1 -> x0, waiting for transfers between devices: 93.6 us -> none  [on_device(): lax.psum(numerator.astype(jnp.bfloat16), 'col').astype(jnp.float32)]
    reduce_sum x38 -> x0, other arithmetic: 73.1 us -> none  [the longest x19 39.9 us: normalize(): average = jnp.mean(values, -1, keepdims=True)]
    pmax x1 -> x0, blocking collectives: 62.1 us -> none  [on_device(): row_peak = lax.pmax(local_peak, 'col')]
    psum x1 -> x0, blocking collectives: 39 us -> none  [on_device(): lax.psum(denominator.astype(jnp.bfloat16), 'col').astype(jnp.float32)]
    convert_element_type x12 -> x0, other arithmetic: 20.4 us -> none  [the longest x8 19 us: one_block(): normed = normalize(middle, pair_gain).astype(jnp.bfloat16).reshape(block_...]
  transfers between devices with their start and end apart: 2 -> 0, of which waited for: 2 -> 0; matrix products, arithmetic and copies ran while one was open for 1% -> 0% of each run, Pallas kernels for 0% -> 0%
where the time goes in v1:
time: 177 us; the launch traced here: 176 us
  Pallas kernels  173 us (98%)
  local copies, waits for them, and re-layouts  2.55 us (1%)
    pallas_call x1, Pallas kernels, main(): pl.pallas_call(functools.partial(main_kernel, head_count, row_devices), g...  141 us
    pallas_call x1, Pallas kernels, gather(): pl.pallas_call(functools.partial(gather_kernel, rows, cols, per_block), o...  18.1 us
    pallas_call x1, Pallas kernels, combine(): pl.pallas_call(functools.partial(combine_kernel, cols, head_count), out_s...  13.7 us

profile of v1, /device:TPU:1, one launch (start us, length us, event | category | flops | bytes accessed | tf_op | source)
XLA Modules:
  0.0 176.3 jit_solution(2355352684526392271)
XLA Ops:
  0.6 1.2 broadcast_in_dim.10.sgain_ref
  1.9 18.1 %gather_tokens.1 = (bf16[256,384]{1,0:T(8,128)(2,1)}, bf16[128,384]{1,0:T(8,128)(2,1)}) custom-call(bf16[16,384]{1,0:T(8,128)(2,1)} %single_ref.3), custom_call_target="tpu_custom_call" | custom-call | tf_op jit(solution)/shard_map/gather_tokens/pallas_call | solution.py:124
  19.9 141.3 %pair_main.1 = (bf16[256,128,128]{2,1,0:T(8,128)(2,1)}, bf16[256,384]{1,0:T(8,128)(2,1)}, f32[256,128]{1,0:T(8,128)}) custom-call(s32[8]{0:T(128)} %seg_ref.1, bf16[256,384]{1,0:T(8,128)(2,1)} %get-tuple-element.7.row_ref, bf16[128,384]{1,0:T(8,128)(2,1)} %get-tuple-element.8.col_ref, f32[1,384]{1,0:T(1,128)} %broadcast_in_dim.10.sgain_ref, ...), custom_call_target="tpu_custom_call" | custom-call | tf_op jit(solution)/shard_map/pair_main/pallas_call | solution.py:280
  161.3 13.7 %combine_parts.1 = bf16[16,384]{1,0:T(8,128)(2,1)} custom-call(bf16[16,384]{1,0:T(8,128)(2,1)} %single_ref.3, f32[1,384]{1,0:T(1,128)} %broadcast_in_dim.10.sgain_ref, bf16[384,384]{1,0:T(8,128)(2,1)} %wga_ref.1, bf16[384,384]{1,0:T(8,128)(2,1)} %wo_ref.3, bf16[256,384]{1,0:T(8,128)(2,1)} %get-tuple-element.9.num_ref, f32[256,128]{1,0:T(8,128)} %get-tuple-element.10.stat_ref), custom_call_target="tpu_custom_call" | custom-call | tf_op jit(solution)/shard_map/combine_parts/pallas_call | solution.py:401
  175.0 1.3 copy.21

commit v2 on v1

--- a/solution.py
+++ b/solution.py
@@ -13,7 +13,7 @@
 BF16 = jnp.bfloat16
 F32 = jnp.float32
 VMEM_SPEC = pl.BlockSpec(memory_space=pltpu.VMEM)
-CHUNK = 4
+GROUP = 4
 BLOCK = 16
 
 
@@ -159,112 +159,193 @@
     wq_ref,
     wk_ref,
     wv_ref,
-    pair_ref,
-    out_ref,
+    pair_hbm,
+    out_hbm,
     num_ref,
     stat_ref,
+    pair_scr,
+    out_scr,
     wo_scr,
     t_scr,
-    right_scr,
+    blocks_scr,
     q_scr,
-    k_scr,
+    kt_scr,
     v_scr,
     wgu_scr,
+    wd_scr,
+    wb_scr,
+    gain_scr,
     live_scr,
-    bias_scr,
+    normed_scr,
+    middle_scr,
+    hidden_scr,
+    new_scr,
+    rstd_scr,
+    num_scr,
+    stat_scr,
+    in_sems,
+    out_sems,
 ):
-    step = pl.program_id(0)
     row_count, width = row_ref.shape
     col_count = col_ref.shape[0]
     outer = wl_ref.shape[0]
     pair_width = wb_ref.shape[1]
     head_dim = width // head_count
     hid = wg_ref.shape[1]
+    block_total = row_count // BLOCK
+    group_total = row_count // GROUP
+    per_block = BLOCK // GROUP
+    tokens = GROUP * col_count
     limit = row_count * row_devices - seg_ref[seg_ref.shape[0] - 1]
 
-    @pl.when(step == 0)
-    def _():
-        row_start = lax.axis_index("row") * row_count
-        col_start = lax.axis_index("col") * col_count
-        row_norm = normalize(row_ref[...].astype(F32), sgain_ref[...]).astype(BF16)
-        col_norm = normalize(col_ref[...].astype(F32), sgain_ref[...]).astype(BF16)
-        row_tokens = row_start + lax.broadcasted_iota(jnp.int32, (row_count, outer), 0)
-        col_tokens = col_start + lax.broadcasted_iota(jnp.int32, (col_count, outer), 0)
-        left = jnp.where(row_tokens < limit, matmul_nt(row_norm, wl_ref[...]), 0.0).astype(BF16)
-        right = jnp.where(col_tokens < limit, matmul_nt(col_norm, wr_ref[...]), 0.0).astype(BF16)
-        right_scr[...] = right
-        q_scr[...] = matmul(row_norm, wq_ref[...]).astype(BF16)
-        k_scr[...] = matmul(col_norm, wk_ref[...]).astype(BF16)
-        v_scr[...] = matmul(col_norm, wv_ref[...]).astype(BF16)
-        wgu_scr[:, :hid] = (wg_ref[...].astype(F32) * 0.5).astype(BF16)
-        wgu_scr[:, hid:] = wu_ref[...]
-        keys = col_start + lax.broadcasted_iota(jnp.int32, (8, col_count), 1)
-        live_scr[...] = (keys < limit).astype(F32)
-        wo_scr[...] = wo_ref[...].astype(F32)
-
-        def table(pair, carry):
-            d = pair * 2
-            w0 = wo_scr[pl.ds(d, outer, stride=outer), :]
-            w1 = wo_scr[pl.ds(d + 1, outer, stride=outer), :]
-            both = matmul(left, jnp.concatenate([w0, w1], axis=1).astype(BF16))
-            t_scr[pl.ds(d, row_count, stride=outer), :] = both[:, :pair_width]
-            t_scr[pl.ds(d + 1, row_count, stride=outer), :] = both[:, pair_width:]
-            return carry
-
-        lax.fori_loop(0, outer // 2, table, 0)
-
-    pgain = pgain_ref[...]
-    bgain = bgain_ref[...]
-
-    def chunk(index, carry):
-        for half in range(CHUNK // 2):
-            first = index * CHUNK + half * 2
-            base = pl.multiple_of((step * BLOCK + first) * outer, 2 * outer)
-            t_pair = t_scr[pl.ds(base, 2 * outer), :]
-            t_cat = jnp.concatenate([t_pair[:outer], t_pair[outer:]], axis=1).astype(BF16)
-            update = matmul(right_scr[...], t_cat)
-            middle = jnp.concatenate(
-                [
-                    pair_ref[first].astype(F32) + update[:, :pair_width],
-                    pair_ref[first + 1].astype(F32) + update[:, pair_width:],
-                ],
-                axis=0,
+    def block_in(b):
+        rows = pl.ds(pl.multiple_of(b * BLOCK, BLOCK), BLOCK)
+        return pltpu.make_async_copy(pair_hbm.at[rows], pair_scr.at[rows], in_sems.at[b])
+
+    def block_out(b):
+        rows = pl.ds(pl.multiple_of(b * BLOCK, BLOCK), BLOCK)
+        return pltpu.make_async_copy(out_scr.at[rows], out_hbm.at[rows], out_sems.at[b])
+
+    for b in range(block_total):
+        block_in(b).start()
+
+    row_start = lax.axis_index("row") * row_count
+    col_start = lax.axis_index("col") * col_count
+    row_norm = normalize(row_ref[...].astype(F32), sgain_ref[...]).astype(BF16)
+    col_norm = normalize(col_ref[...].astype(F32), sgain_ref[...]).astype(BF16)
+    row_tokens = row_start + lax.broadcasted_iota(jnp.int32, (row_count, outer), 0)
+    col_tokens = col_start + lax.broadcasted_iota(jnp.int32, (outer, col_count), 1)
+    left = jnp.where(row_tokens < limit, matmul_nt(row_norm, wl_ref[...]), 0.0).astype(BF16)
+    right = jnp.where(col_tokens < limit, matmul_nt(wr_ref[...], col_norm), 0.0)
+    q_scr[...] = matmul(row_norm, wq_ref[...]).astype(BF16).astype(F32).reshape(q_scr.shape)
+    kt_scr[...] = matmul(col_norm, wk_ref[...]).astype(BF16).T
+    v_scr[...] = matmul(col_norm, wv_ref[...]).astype(BF16)
+    tall = jnp.broadcast_to(right.astype(BF16).astype(F32)[:, None, :], (outer, 8, col_count))
+    sub = lax.broadcasted_iota(jnp.int32, (outer, 8, col_count), 1)
+    for half in range(8 // GROUP):
+        for r in range(GROUP):
+            picked = jnp.where(sub == half * GROUP + r, tall, 0.0)
+            blocks_scr[half, :, r * col_count : (r + 1) * col_count] = picked.reshape(
+                outer * 8, col_count
+            ).astype(BF16)
+    gate_t = (wg_ref[...].astype(F32) * 0.5).astype(BF16).T
+    up_t = wu_ref[...].T
+    for m in range(hid // 16):
+        wgu_scr[32 * m : 32 * m + 16, :] = gate_t[16 * m : 16 * m + 16]
+        wgu_scr[32 * m + 16 : 32 * m + 32, :] = up_t[16 * m : 16 * m + 16]
+    wd_scr[...] = wd_ref[...].T
+    scaled = wb_ref[...].astype(F32) * bgain_ref[...]
+    scaled = scaled - jnp.mean(scaled, -1, keepdims=True)
+    high = scaled.astype(BF16)
+    wb_scr[:head_count] = high
+    wb_scr[head_count:] = (scaled - high.astype(F32)).astype(BF16)
+    gain_scr[...] = jnp.broadcast_to(pgain_ref[...], (col_count, pair_width)).T
+    keys = col_start + lax.broadcasted_iota(jnp.int32, (8, col_count), 1)
+    live_scr[...] = (keys < limit).astype(F32)
+    wo_scr[...] = wo_ref[...].astype(F32)
+
+    def table(pair, carry):
+        d = pair * 2
+        w0 = wo_scr[pl.ds(d, outer, stride=outer), :]
+        w1 = wo_scr[pl.ds(d + 1, outer, stride=outer), :]
+        both = matmul(left, jnp.concatenate([w0, w1], axis=1).astype(BF16))
+        t_scr[d] = both[:, :pair_width]
+        t_scr[d + 1] = both[:, pair_width:]
+        return carry
+
+    lax.fori_loop(0, outer // 2, table, 0)
+
+    own_head = (
+        lax.broadcasted_iota(jnp.int32, (GROUP, head_count, width), 2) // head_dim
+        == lax.broadcasted_iota(jnp.int32, (GROUP, head_count, width), 1)
+    )
+    lane = lax.broadcasted_iota(jnp.int32, (GROUP, head_count, 128), 2)
+    head = lax.broadcasted_iota(jnp.int32, (GROUP, head_count, 128), 1)
+
+    def lanes(r):
+        return slice(r * col_count, (r + 1) * col_count)
+
+    def attend(group):
+        pieces = matmul(wb_scr[...], new_scr[...])
+        bias = (pieces[:head_count] + pieces[head_count:]) * rstd_scr[0:1, :]
+        bias = jnp.concatenate([bias[:, lanes(r)] for r in range(GROUP)], axis=0)
+        query = q_scr[group]
+        spread = jnp.where(own_head, query[:, None, :], 0.0)
+        spread = spread.reshape(GROUP * head_count, width).astype(BF16)
+        scores = matmul(spread, kt_scr[...]) * (1.0 / math.sqrt(head_dim)) + bias
+        scores = jnp.where(live_scr[0:1, :] > 0.0, scores, -1e30)
+        peak = jnp.max(scores, -1, keepdims=True)
+        weights = jnp.exp(scores - peak)
+        total = jnp.sum(weights, -1, keepdims=True)
+        full = matmul(weights.astype(BF16), v_scr[...]).reshape(GROUP, head_count, width)
+        num_scr[group] = jnp.sum(jnp.where(own_head, full, 0.0), axis=1)
+        wide = (GROUP * head_count, 128)
+        peaks = jnp.broadcast_to(peak, wide).reshape(lane.shape)
+        totals = jnp.broadcast_to(total, wide).reshape(lane.shape)
+        stats = jnp.where(lane == head, peaks, jnp.where(lane == head + head_count, totals, 0.0))
+        stat_scr[group] = jnp.sum(stats, axis=1)
+
+    def project(group, slot):
+        down = matmul(wd_scr[...], hidden_scr[...])
+        for r in range(GROUP):
+            new_pair = (middle_scr[slot, :, lanes(r)] + down[:, lanes(r)]).astype(BF16)
+            out_scr[group * GROUP + r] = new_pair.T
+            new_scr[:, lanes(r)] = new_pair
+            wide = new_pair.astype(F32)
+            centered = wide - jnp.mean(wide, axis=0, keepdims=True)
+            variance = jnp.mean(centered * centered, axis=0, keepdims=True)
+            rstd_scr[:, lanes(r)] = jnp.broadcast_to(
+                lax.rsqrt(variance + EPSILON), (8, col_count)
             )
-            normed = normalize(middle, pgain).astype(BF16)
-            both = matmul(normed, wgu_scr[...])
-            half_gate, up = both[:, :hid], both[:, hid:]
-            hidden = ((half_gate * jnp.tanh(half_gate) + half_gate) * up).astype(BF16)
-            new_pair = (middle + matmul(hidden, wd_ref[...])).astype(BF16)
-            out_ref[first] = new_pair[:col_count]
-            out_ref[first + 1] = new_pair[col_count:]
-            bias_input = normalize(new_pair.astype(F32), bgain).astype(BF16)
-            bias = matmul_nt(wb_ref[...], bias_input)
-            at = pl.multiple_of(first * head_count, 2 * head_count)
-            bias_scr[pl.ds(at, 2 * head_count), :] = jnp.concatenate(
-                [bias[:, :col_count], bias[:, col_count:]], axis=0
-            )
+
+    def expand():
+        both = matmul(wgu_scr[...], normed_scr[...])
+        for m in range(hid // 16):
+            half_gate, up = both[32 * m : 32 * m + 16], both[32 * m + 16 : 32 * m + 32]
+            hidden = (half_gate * jnp.tanh(half_gate) + half_gate) * up
+            hidden_scr[16 * m : 16 * m + 16, :] = hidden.astype(BF16)
+
+    def update(group, slot):
+        rows = pl.ds(pl.multiple_of(group // (8 // GROUP) * 8, 8), 8)
+        table_t = t_scr[:, rows, :].reshape(outer * 8, pair_width).astype(BF16).T
+        added = matmul(table_t, blocks_scr[lax.rem(group, 8 // GROUP)])
+        for r in range(GROUP):
+            middle = pair_scr[group * GROUP + r].T.astype(F32) + added[:, lanes(r)]
+            middle_scr[slot, :, lanes(r)] = middle
+            centered = middle - jnp.mean(middle, axis=0, keepdims=True)
+            variance = jnp.mean(centered * centered, axis=0, keepdims=True)
+            normed = centered * lax.rsqrt(variance + EPSILON) * gain_scr[...]
+            normed_scr[:, lanes(r)] = normed.astype(BF16)
+
+    def clamp(group):
+        return jnp.clip(group, 0, group_total - 1)
+
+    def step(s, carry):
+        slot = lax.rem(s, 2)
+        attend(clamp(s - 3))
+        project(clamp(s - 2), slot)
+        expand()
+        update(clamp(s), slot)
         return carry
 
-    lax.fori_loop(0, BLOCK // CHUNK, chunk, 0)
-
-    pairs = BLOCK * head_count
-    query = q_scr[pl.ds(pl.multiple_of(step * BLOCK, BLOCK), BLOCK), :].astype(F32)
-    head_of = lax.broadcasted_iota(jnp.int32, (BLOCK, head_count, width), 2) // head_dim
-    own_head = head_of == lax.broadcasted_iota(jnp.int32, (BLOCK, head_count, width), 1)
-    spread = jnp.where(own_head, query[:, None, :], 0.0).reshape(pairs, width).astype(BF16)
-    scores = matmul_nt(spread, k_scr[...]) * (1.0 / math.sqrt(head_dim)) + bias_scr[...]
-    scores = jnp.where(live_scr[0:1, :] > 0.0, scores, -1e30)
-    peak = jnp.max(scores, -1, keepdims=True)
-    weights = jnp.exp(scores - peak)
-    total = jnp.sum(weights, -1, keepdims=True)
-    full = matmul(weights.astype(BF16), v_scr[...]).reshape(BLOCK, head_count, width)
-    num_ref[...] = jnp.sum(jnp.where(own_head, full, 0.0), axis=1).astype(BF16)
-    lane = lax.broadcasted_iota(jnp.int32, (BLOCK, head_count, 128), 2)
-    head = lax.broadcasted_iota(jnp.int32, (BLOCK, head_count, 128), 1)
-    peak_b = jnp.broadcast_to(peak, (pairs, 128)).reshape(BLOCK, head_count, 128)
-    total_b = jnp.broadcast_to(total, (pairs, 128)).reshape(BLOCK, head_count, 128)
-    stats = jnp.where(lane == head, peak_b, jnp.where(lane == head + head_count, total_b, 0.0))
-    stat_ref[...] = jnp.sum(stats, axis=1)
+    block_in(0).wait()
+
+    def block(b, carry):
+        @pl.when(b + 1 < block_total)
+        def _():
+            block_in(b + 1).wait()
+
+        first = jnp.where(b == 0, 0, per_block * b + 2)
+        last = per_block * b + per_block + 2 + jnp.where(b == block_total - 1, 1, 0)
+        lax.fori_loop(first, last, step, 0)
+        block_out(b).start()
+        return carry
+
+    lax.fori_loop(0, block_total, block, 0)
+    num_ref[...] = num_scr[...].reshape(row_count, width).astype(BF16)
+    stat_ref[...] = stat_scr[...].reshape(row_count, 128)
+    for b in range(block_total):
+        block_out(b).wait()
 
 
 def main(head_count, row_devices, seg, row_tokens, col_tokens, weights, pair_input):
@@ -272,14 +353,10 @@
     width = row_tokens.shape[1]
     outer = weights[1].shape[0]
     hid = weights[5].shape[1]
-
-    def whole(array):
-        return pl.BlockSpec(array.shape, lambda i: (0,) * array.ndim, pipeline_mode=pl.Buffered(1))
-
-    pair_spec = pl.BlockSpec((BLOCK, col_count, pair_width), lambda i: (i, 0, 0))
+    tokens = GROUP * col_count
+    any_spec = pl.BlockSpec(memory_space=pl.ANY)
     return pl.pallas_call(
         functools.partial(main_kernel, head_count, row_devices),
-        grid=(row_count // BLOCK,),
         out_shape=(
             jax.ShapeDtypeStruct(pair_input.shape, BF16),
             jax.ShapeDtypeStruct((row_count, width), BF16),
@@ -287,30 +364,35 @@
         ),
         in_specs=[
             pl.BlockSpec(memory_space=pltpu.SMEM),
-            whole(row_tokens),
-            whole(col_tokens),
-            *[whole(w) for w in weights],
-            pair_spec,
+            *([VMEM_SPEC] * (2 + len(weights))),
+            any_spec,
         ],
-        out_specs=(
-            pair_spec,
-            pl.BlockSpec((BLOCK, width), lambda i: (i, 0)),
-            pl.BlockSpec((BLOCK, 128), lambda i: (i, 0)),
-        ),
+        out_specs=(any_spec, VMEM_SPEC, VMEM_SPEC),
         scratch_shapes=[
+            pltpu.VMEM(pair_input.shape, BF16),
+            pltpu.VMEM(pair_input.shape, BF16),
             pltpu.VMEM((outer * outer, pair_width), F32),
-            pltpu.VMEM((row_count * outer, pair_width), F32),
-            pltpu.VMEM((col_count, outer), BF16),
-            pltpu.VMEM((row_count, width), BF16),
+            pltpu.VMEM((outer, row_count, pair_width), F32),
+            pltpu.VMEM((8 // GROUP, outer * 8, tokens), BF16),
+            pltpu.VMEM((row_count // GROUP, GROUP, width), F32),
+            pltpu.VMEM((width, col_count), BF16),
             pltpu.VMEM((col_count, width), BF16),
-            pltpu.VMEM((col_count, width), BF16),
-            pltpu.VMEM((pair_width, 2 * hid), BF16),
+            pltpu.VMEM((2 * hid, pair_width), BF16),
+            pltpu.VMEM((pair_width, hid), BF16),
+            pltpu.VMEM((2 * head_count, pair_width), BF16),
+            pltpu.VMEM((pair_width, col_count), F32),
             pltpu.VMEM((8, col_count), F32),
-            pltpu.VMEM((BLOCK * head_count, col_count), F32),
+            pltpu.VMEM((pair_width, tokens), BF16),
+            pltpu.VMEM((2, pair_width, tokens), F32),
+            pltpu.VMEM((hid, tokens), BF16),
+            pltpu.VMEM((pair_width, tokens), BF16),
+            pltpu.VMEM((8, tokens), F32),
+            pltpu.VMEM((row_count // GROUP, GROUP, width), F32),
+            pltpu.VMEM((row_count // GROUP, GROUP, 128), F32),
+            pltpu.SemaphoreType.DMA((row_count // BLOCK,)),
+            pltpu.SemaphoreType.DMA((row_count // BLOCK,)),
         ],
-        compiler_params=pltpu.CompilerParams(
-            dimension_semantics=("arbitrary",), vmem_limit_bytes=56 << 20
-        ),
+        compiler_params=pltpu.CompilerParams(vmem_limit_bytes=56 << 20),
         name="pair_main",
     )(seg, row_tokens, col_tokens, *weights, pair_input)
 

time: 177 us -> 104 us (0.59)
  Pallas kernels: 173 us -> 101 us
    pallas_call x1, Pallas kernels: 141 us -> 69.1 us  [main(): pl.pallas_call(functools.partial(main_kernel, head_count, row_devices), o...]
where the time goes in v2:
time: 104 us
  Pallas kernels  101 us (97%)
  local copies, waits for them, and re-layouts  2.55 us (2%)
    pallas_call x1, Pallas kernels, main(): pl.pallas_call(functools.partial(main_kernel, head_count, row_devices), o...  69.1 us
    pallas_call x1, Pallas kernels, gather(): pl.pallas_call(functools.partial(gather_kernel, rows, cols, per_block), o...  18.1 us
    pallas_call x1, Pallas kernels, combine(): pl.pallas_call(functools.partial(combine_kernel, cols, head_count), out_s...  13.7 us

profile of v2, /device:TPU:1, one launch (start us, length us, event | category | flops | bytes accessed | tf_op | source)
XLA Modules:
  0.0 104.0 jit_solution(8502966904951458946)
XLA Ops:
  0.6 1.2 %broadcast_in_dim.10.sgain_ref = f32[1,384]{1,0:T(1,128)} reshape(f32[384]{0:T(512)} %param.21) | data formatting | bytes 3072 | tf_op jit(solution)/shard_map/broadcast_in_dim | solution.py:545
  1.9 18.1 %gather_tokens.1 = (bf16[256,384]{1,0:T(8,128)(2,1)}, bf16[128,384]{1,0:T(8,128)(2,1)}) custom-call(bf16[16,384]{1,0:T(8,128)(2,1)} %single_ref.3), custom_call_target="tpu_custom_call" | custom-call | tf_op jit(solution)/shard_map/gather_tokens/pallas_call | solution.py:124
  19.9 69.1 %pair_main.1 = (bf16[256,128,128]{2,1,0:T(8,128)(2,1)}, bf16[256,384]{1,0:T(8,128)(2,1)}, f32[256,128]{1,0:T(8,128)}) custom-call(s32[8]{0:T(128)} %seg_ref.1, bf16[256,384]{1,0:T(8,128)(2,1)} %get-tuple-element.7.row_ref, bf16[128,384]{1,0:T(8,128)(2,1)} %get-tuple-element.8.col_ref, f32[1,384]{1,0:T(1,128)} %broadcast_in_dim.10.sgain_ref, ...), custom_call_target="tpu_custom_call" | custom-call | tf_op jit(solution)/shard_map/pair_main/pallas_call | solution.py:358
  89.0 13.7 %combine_parts.1 = bf16[16,384]{1,0:T(8,128)(2,1)} custom-call(bf16[16,384]{1,0:T(8,128)(2,1)} %single_ref.3, f32[1,384]{1,0:T(1,128)} %broadcast_in_dim.10.sgain_ref, bf16[384,384]{1,0:T(8,128)(2,1)} %wga_ref.1, bf16[384,384]{1,0:T(8,128)(2,1)} %wo_ref.3, bf16[256,384]{1,0:T(8,128)(2,1)} %get-tuple-element.9.num_ref, f32[256,128]{1,0:T(8,128)} %get-tuple-element.10.stat_ref), custom_call_target="tpu_custom_call" | custom-call | tf_op jit(solution)/shard_map/combine_parts/pallas_call | solution.py:483
  102.7 1.3 %copy.21 = bf16[16,384]{1,0:T(8,128)(2,1)} copy(bf16[16,384]{1,0:T(8,128)(2,1)} %combine_parts.1) | data formatting | bytes 24576

commit v3 on v2

--- a/solution.py
+++ b/solution.py
@@ -260,14 +260,15 @@
         == lax.broadcasted_iota(jnp.int32, (GROUP, head_count, width), 1)
     )
     lane = lax.broadcasted_iota(jnp.int32, (GROUP, head_count, 128), 2)
-    head = lax.broadcasted_iota(jnp.int32, (GROUP, head_count, 128), 1)
+    place = lax.broadcasted_iota(jnp.int32, (GROUP, head_count, 128), 1)
+    place = place + lax.broadcasted_iota(jnp.int32, lane.shape, 0) * (2 * head_count)
 
     def lanes(r):
         return slice(r * col_count, (r + 1) * col_count)
 
-    def attend(group):
-        pieces = matmul(wb_scr[...], new_scr[...])
-        bias = (pieces[:head_count] + pieces[head_count:]) * rstd_scr[0:1, :]
+    def score(group, owner, at, part):
+        pieces = matmul(wb_scr[...], new_scr[part])
+        bias = (pieces[:head_count] + pieces[head_count:]) * rstd_scr[part, 0:1, :]
         bias = jnp.concatenate([bias[:, lanes(r)] for r in range(GROUP)], axis=0)
         query = q_scr[group]
         spread = jnp.where(own_head, query[:, None, :], 0.0)
@@ -277,73 +278,86 @@
         peak = jnp.max(scores, -1, keepdims=True)
         weights = jnp.exp(scores - peak)
         total = jnp.sum(weights, -1, keepdims=True)
-        full = matmul(weights.astype(BF16), v_scr[...]).reshape(GROUP, head_count, width)
-        num_scr[group] = jnp.sum(jnp.where(own_head, full, 0.0), axis=1)
         wide = (GROUP * head_count, 128)
         peaks = jnp.broadcast_to(peak, wide).reshape(lane.shape)
         totals = jnp.broadcast_to(total, wide).reshape(lane.shape)
-        stats = jnp.where(lane == head, peaks, jnp.where(lane == head + head_count, totals, 0.0))
-        stat_scr[group] = jnp.sum(stats, axis=1)
-
-    def project(group, slot):
-        down = matmul(wd_scr[...], hidden_scr[...])
+        stats = jnp.where(lane == place, peaks, 0.0)
+        stats = jnp.where(lane == place + head_count, totals, stats)
+        stats = jnp.sum(jnp.sum(stats, axis=0), axis=0, keepdims=True)
+        stat_scr[owner, at : at + 1, :] = stats
+        return weights.astype(BF16)
+
+    def collect(owner, at, weights):
+        full = matmul(weights, v_scr[...]).reshape(GROUP, head_count, width)
+        rows = jnp.sum(jnp.where(own_head, full, 0.0), axis=1)
         for r in range(GROUP):
-            new_pair = (middle_scr[slot, :, lanes(r)] + down[:, lanes(r)]).astype(BF16)
+            num_scr[owner, at : at + 1, r * width : (r + 1) * width] = rows[r : r + 1]
+
+    def project(group, part):
+        down = matmul(wd_scr[...], hidden_scr[part])
+        for r in range(GROUP):
+            wide = middle_scr[part, :, lanes(r)] + down[:, lanes(r)]
+            new_pair = wide.astype(BF16)
             out_scr[group * GROUP + r] = new_pair.T
-            new_scr[:, lanes(r)] = new_pair
-            wide = new_pair.astype(F32)
+            new_scr[part, :, lanes(r)] = new_pair
             centered = wide - jnp.mean(wide, axis=0, keepdims=True)
             variance = jnp.mean(centered * centered, axis=0, keepdims=True)
-            rstd_scr[:, lanes(r)] = jnp.broadcast_to(
+            rstd_scr[part, :, lanes(r)] = jnp.broadcast_to(
                 lax.rsqrt(variance + EPSILON), (8, col_count)
             )
 
-    def expand():
-        both = matmul(wgu_scr[...], normed_scr[...])
-        for m in range(hid // 16):
+    def expand(index, count, part):
+        size = hid // count
+        both = matmul(wgu_scr[2 * index * size : 2 * (index + 1) * size], normed_scr[part])
+        base = index * size
+        for m in range(size // 16):
             half_gate, up = both[32 * m : 32 * m + 16], both[32 * m + 16 : 32 * m + 32]
             hidden = (half_gate * jnp.tanh(half_gate) + half_gate) * up
-            hidden_scr[16 * m : 16 * m + 16, :] = hidden.astype(BF16)
-
-    def update(group, slot):
+            hidden_scr[part, base + 16 * m : base + 16 * m + 16, :] = hidden.astype(BF16)
+
+    def update(group, part):
         rows = pl.ds(pl.multiple_of(group // (8 // GROUP) * 8, 8), 8)
         table_t = t_scr[:, rows, :].reshape(outer * 8, pair_width).astype(BF16).T
         added = matmul(table_t, blocks_scr[lax.rem(group, 8 // GROUP)])
         for r in range(GROUP):
             middle = pair_scr[group * GROUP + r].T.astype(F32) + added[:, lanes(r)]
-            middle_scr[slot, :, lanes(r)] = middle
+            middle_scr[part, :, lanes(r)] = middle
             centered = middle - jnp.mean(middle, axis=0, keepdims=True)
             variance = jnp.mean(centered * centered, axis=0, keepdims=True)
             normed = centered * lax.rsqrt(variance + EPSILON) * gain_scr[...]
-            normed_scr[:, lanes(r)] = normed.astype(BF16)
+            normed_scr[part, :, lanes(r)] = normed.astype(BF16)
 
     def clamp(group):
         return jnp.clip(group, 0, group_total - 1)
 
-    def step(s, carry):
-        slot = lax.rem(s, 2)
-        attend(clamp(s - 3))
-        project(clamp(s - 2), slot)
-        expand()
-        update(clamp(s), slot)
+    def block(b, carry):
+        @pl.when(b < block_total)
+        def _():
+            block_in(b).wait()
+
+        for u in range(per_block):
+            s = b * per_block + u
+            part = u % 2
+            owner = jnp.maximum(b - 1, 0) if u < 3 else b
+            at = (u + 1) % per_block
+            weights = score(clamp(s - 3), owner, at, 1 - part)
+            expand(0, 4, 1 - part)
+            project(clamp(s - 2), part)
+            expand(1, 4, 1 - part)
+            update(clamp(s), part)
+            expand(2, 4, 1 - part)
+            collect(owner, at, weights)
+            expand(3, 4, 1 - part)
+
+        @pl.when(b > 0)
+        def _():
+            block_out(b - 1).start()
+
         return carry
 
-    block_in(0).wait()
-
-    def block(b, carry):
-        @pl.when(b + 1 < block_total)
-        def _():
-            block_in(b + 1).wait()
-
-        first = jnp.where(b == 0, 0, per_block * b + 2)
-        last = per_block * b + per_block + 2 + jnp.where(b == block_total - 1, 1, 0)
-        lax.fori_loop(first, last, step, 0)
-        block_out(b).start()
-        return carry
-
-    lax.fori_loop(0, block_total, block, 0)
-    num_ref[...] = num_scr[...].reshape(row_count, width).astype(BF16)
-    stat_ref[...] = stat_scr[...].reshape(row_count, 128)
+    lax.fori_loop(0, block_total + 1, block, 0)
+    num_ref[...] = num_scr[:block_total].astype(BF16)
+    stat_ref[...] = stat_scr[:block_total]
     for b in range(block_total):
         block_out(b).wait()
 
@@ -359,8 +373,8 @@
         functools.partial(main_kernel, head_count, row_devices),
         out_shape=(
             jax.ShapeDtypeStruct(pair_input.shape, BF16),
-            jax.ShapeDtypeStruct((row_count, width), BF16),
-            jax.ShapeDtypeStruct((row_count, 128), F32),
+            jax.ShapeDtypeStruct((row_count // BLOCK, BLOCK // GROUP, GROUP * width), BF16),
+            jax.ShapeDtypeStruct((row_count // BLOCK, BLOCK // GROUP, 128), F32),
         ),
         in_specs=[
             pl.BlockSpec(memory_space=pltpu.SMEM),
@@ -382,13 +396,13 @@
             pltpu.VMEM((2 * head_count, pair_width), BF16),
             pltpu.VMEM((pair_width, col_count), F32),
             pltpu.VMEM((8, col_count), F32),
-            pltpu.VMEM((pair_width, tokens), BF16),
+            pltpu.VMEM((2, pair_width, tokens), BF16),
             pltpu.VMEM((2, pair_width, tokens), F32),
-            pltpu.VMEM((hid, tokens), BF16),
-            pltpu.VMEM((pair_width, tokens), BF16),
-            pltpu.VMEM((8, tokens), F32),
-            pltpu.VMEM((row_count // GROUP, GROUP, width), F32),
-            pltpu.VMEM((row_count // GROUP, GROUP, 128), F32),
+            pltpu.VMEM((2, hid, tokens), BF16),
+            pltpu.VMEM((2, pair_width, tokens), BF16),
+            pltpu.VMEM((2, 8, tokens), F32),
+            pltpu.VMEM((row_count // BLOCK + 1, BLOCK // GROUP, GROUP * width), F32),
+            pltpu.VMEM((row_count // BLOCK + 1, BLOCK // GROUP, 128), F32),
             pltpu.SemaphoreType.DMA((row_count // BLOCK,)),
             pltpu.SemaphoreType.DMA((row_count // BLOCK,)),
         ],
@@ -409,6 +423,8 @@
     out_ref,
     nums,
     stats,
+    spread_scr,
+    attended_scr,
     send_num,
     send_stat,
     recv_num,
@@ -416,6 +432,7 @@
 ):
     own, width = single_ref.shape
     head_dim = width // head_count
+    groups = own // GROUP
     row, col = lax.axis_index("row"), lax.axis_index("col")
 
     barrier = pltpu.get_barrier_semaphore()
@@ -425,53 +442,65 @@
         )
     single = single_ref[...].astype(F32)
     gate = matmul(normalize(single, sgain_ref[...]).astype(BF16), wga_ref[...])
+    gate = jax.nn.sigmoid(gate)
+    lane = lax.rem(lax.broadcasted_iota(jnp.int32, (256, width), 0), 128)
+    head = lax.broadcasted_iota(jnp.int32, (256, width), 1) // head_dim
+    for r in range(GROUP):
+        spread_scr[:, r * width : (r + 1) * width] = jnp.where(
+            lane == head + r * 2 * head_count, 1.0, 0.0
+        ).astype(BF16)
     pl.semaphore_wait(barrier, cols - 1)
 
     def copies(step):
         peer = lax.rem(col + step, cols)
-        block = pl.ds(pl.multiple_of(peer * own, own), own)
         return (
             pltpu.make_async_remote_copy(
-                src_ref=num_ref.at[block],
+                src_ref=stat_ref.at[peer],
+                dst_ref=stats.at[col],
+                send_sem=send_stat.at[step],
+                recv_sem=recv_stat.at[col],
+                device_id=(row, peer),
+                device_id_type=MESH,
+            ),
+            pltpu.make_async_remote_copy(
+                src_ref=num_ref.at[peer],
                 dst_ref=nums.at[col],
                 send_sem=send_num.at[step],
                 recv_sem=recv_num.at[col],
                 device_id=(row, peer),
                 device_id_type=MESH,
             ),
-            pltpu.make_async_remote_copy(
-                src_ref=stat_ref.at[block],
-                dst_ref=stats.at[col],
-                send_sem=send_stat.at[step],
-                recv_sem=recv_stat.at[col],
-                device_id=(row, peer),
-                device_id_type=MESH,
-            ),
         )
 
     for step in range(1, cols):
         for copy in copies(step):
             copy.start()
-    block = pl.ds(pl.multiple_of(col * own, own), own)
-    pltpu.make_async_copy(num_ref.at[block], nums.at[col], recv_num.at[col]).start()
-    pltpu.make_async_copy(stat_ref.at[block], stats.at[col], recv_stat.at[col]).start()
+    pltpu.make_async_copy(num_ref.at[col], nums.at[col], recv_num.at[col]).start()
+    pltpu.make_async_copy(stat_ref.at[col], stats.at[col], recv_stat.at[col]).start()
     for sender in range(cols):
-        pltpu.make_async_copy(nums.at[sender], nums.at[sender], recv_num.at[sender]).wait()
         pltpu.make_async_copy(stats.at[sender], stats.at[sender], recv_stat.at[sender]).wait()
 
     part = stats[...]
     top = jnp.max(part, axis=0)
     scale = jnp.exp(part - top[None])
     total = jnp.sum(scale * pltpu.roll(part, 128 - head_count, 2), axis=0)
-    lane = lax.broadcasted_iota(jnp.int32, (128, width), 0)
-    spread = (lane == lax.broadcasted_iota(jnp.int32, (128, width), 1) // head_dim).astype(F32)
-    head_lane = lax.broadcasted_iota(jnp.int32, (own, 128), 1) < head_count
-    share = jnp.where(head_lane[None], scale / total[None], 0.0).reshape(cols * own, 128)
-    wide = jnp.dot(
-        share, spread, precision=lax.Precision.HIGHEST, preferred_element_type=F32
-    ).reshape(cols, own, width)
+    peak_lane = lax.rem(lax.broadcasted_iota(jnp.int32, (groups, 128), 1), 2 * head_count)
+    share = jnp.where((peak_lane < head_count)[None], scale / total[None], 0.0)
+    share = share.reshape(cols * groups, 128)
+    high = share.astype(BF16)
+    low = (share - high.astype(F32)).astype(BF16)
+    wide = matmul(jnp.concatenate([high, low], axis=1), spread_scr[...])
+    wide = wide.reshape(cols, groups, GROUP * width)
+    for sender in range(cols):
+        pltpu.make_async_copy(nums.at[sender], nums.at[sender], recv_num.at[sender]).wait()
     attended = jnp.sum(wide * nums[...].astype(F32), axis=0)
-    gated = (jax.nn.sigmoid(gate) * attended).astype(BF16)
+    for g in range(groups):
+        for r in range(GROUP):
+            token = g * GROUP + r
+            attended_scr[token : token + 1, :] = attended[
+                g : g + 1, r * width : (r + 1) * width
+            ]
+    gated = (gate * attended_scr[...]).astype(BF16)
     out_ref[...] = (single + matmul(gated, wo_ref[...])).astype(BF16)
     for step in range(1, cols):
         for copy in copies(step):
@@ -486,8 +515,10 @@
         in_specs=[VMEM_SPEC] * 6,
         out_specs=VMEM_SPEC,
         scratch_shapes=[
-            pltpu.VMEM((cols, own, width), BF16),
-            pltpu.VMEM((cols, own, 128), F32),
+            pltpu.VMEM((cols, *num.shape[1:]), BF16),
+            pltpu.VMEM((cols, *stat.shape[1:]), F32),
+            pltpu.VMEM((256, GROUP * width), BF16),
+            pltpu.VMEM((own, width), F32),
             pltpu.SemaphoreType.DMA((cols,)),
             pltpu.SemaphoreType.DMA((cols,)),
             pltpu.SemaphoreType.DMA((cols,)),
@@ -524,7 +555,7 @@
     head_count = w_bias.shape[1]
     row_tokens, col_tokens = gather(single, rows, cols, row_count, col_count)
     weights = (
-        single_gain[None, :],
+        single_gain,
         w_left.T,
         w_right.T,
         w_outer,
@@ -542,7 +573,7 @@
         head_count, rows, segment_lengths, row_tokens, col_tokens, weights, pair_input
     )
     single_out = combine(
-        cols, head_count, single, single_gain[None, :], w_gate_attn, w_output, num, stat
+        cols, head_count, single, single_gain, w_gate_attn, w_output, num, stat
     )
     return (single_out, pair_out)
 

time: 104 us -> 78.4 us (0.75)
  Pallas kernels: 101 us -> 76.2 us
  local copies, waits for them, and re-layouts: 2.55 us -> 1.31 us
    pallas_call x1, Pallas kernels: 69.1 us -> 45.3 us  [main(): pl.pallas_call(functools.partial(main_kernel, head_count, row_devices), o...]
    broadcast_in_dim x1 -> x0, local copies, waits for them, and re-layouts: 1.25 us -> none  [on_device(): single_gain[None, :]]
where the time goes in v3:
time: 78.4 us; the launch traced here: 78.1 us
  Pallas kernels  76.2 us (97%)
  local copies, waits for them, and re-layouts  1.31 us (2%)
    pallas_call x1, Pallas kernels, main(): pl.pallas_call(functools.partial(main_kernel, head_count, row_devices), o...  45.3 us
    pallas_call x1, Pallas kernels, gather(): pl.pallas_call(functools.partial(gather_kernel, rows, cols, per_block), o...  18.1 us
    pallas_call x1, Pallas kernels, combine(): pl.pallas_call(functools.partial(combine_kernel, cols, head_count), out_s...  12.8 us

profile of v3, /device:TPU:1, one launch (start us, length us, event | category | flops | bytes accessed | tf_op | source)
XLA Modules:
  0.0 78.1 jit_solution(789890886253845020)
XLA Ops:
  0.6 18.1 %gather_tokens.1 = (bf16[256,384]{1,0:T(8,128)(2,1)}, bf16[128,384]{1,0:T(8,128)(2,1)}) custom-call(bf16[16,384]{1,0:T(8,128)(2,1)} %single_ref.3), custom_call_target="tpu_custom_call" | custom-call | tf_op jit(solution)/shard_map/gather_tokens/pallas_call | solution.py:124
  18.8 45.3 %pair_main.1 = (bf16[256,128,128]{2,1,0:T(8,128)(2,1)}, bf16[16,4,1536]{2,1,0:T(4,128)(2,1)}, f32[16,4,128]{2,1,0:T(4,128)}) custom-call(s32[8]{0:T(128)} %seg_ref.1, bf16[256,384]{1,0:T(8,128)(2,1)} %get-tuple-element.7.row_ref, bf16[128,384]{1,0:T(8,128)(2,1)} %get-tuple-element.8.col_ref, f32[384]{0:T(512)} %sgain_ref.3, bf16[32,384]{1,0:T(8,128)(2,1)} %bitcast.5, ...), custom_call_target="tpu_custom_call" | custom-call | tf_op jit(solution)/shard_map/pair_main/pallas_call | solution.py:372
  64.0 12.8 %combine_parts.1 = bf16[16,384]{1,0:T(8,128)(2,1)} custom-call(bf16[16,384]{1,0:T(8,128)(2,1)} %single_ref.3, f32[384]{0:T(512)} %sgain_ref.3, bf16[384,384]{1,0:T(8,128)(2,1)} %wga_ref.1, bf16[384,384]{1,0:T(8,128)(2,1)} %wo_ref.3, bf16[16,4,1536]{2,1,0:T(4,128)(2,1)} %get-tuple-element.9.num_ref, f32[16,4,128]{2,1,0:T(4,128)} %get-tuple-element.10.stat_ref), custom_call_target="tpu_custom_call" | custom-call | tf_op jit(solution)/shard_map/combine_parts/pallas_call | solution.py:512
  76.8 1.3 %copy.21 = bf16[16,384]{1,0:T(8,128)(2,1)} copy(bf16[16,384]{1,0:T(8,128)(2,1)} %combine_parts.1) | data formatting | bytes 24576

commit v4 on v3

--- a/solution.py
+++ b/solution.py
@@ -174,7 +174,7 @@
     wgu_scr,
     wd_scr,
     wb_scr,
-    gain_scr,
+    eye_scr,
     live_scr,
     normed_scr,
     middle_scr,
@@ -195,7 +195,6 @@
     block_total = row_count // BLOCK
     group_total = row_count // GROUP
     per_block = BLOCK // GROUP
-    tokens = GROUP * col_count
     limit = row_count * row_devices - seg_ref[seg_ref.shape[0] - 1]
 
     def block_in(b):
@@ -220,16 +219,20 @@
     q_scr[...] = matmul(row_norm, wq_ref[...]).astype(BF16).astype(F32).reshape(q_scr.shape)
     kt_scr[...] = matmul(col_norm, wk_ref[...]).astype(BF16).T
     v_scr[...] = matmul(col_norm, wv_ref[...]).astype(BF16)
-    tall = jnp.broadcast_to(right.astype(BF16).astype(F32)[:, None, :], (outer, 8, col_count))
-    sub = lax.broadcasted_iota(jnp.int32, (outer, 8, col_count), 1)
-    for half in range(8 // GROUP):
-        for r in range(GROUP):
-            picked = jnp.where(sub == half * GROUP + r, tall, 0.0)
-            blocks_scr[half, :, r * col_count : (r + 1) * col_count] = picked.reshape(
-                outer * 8, col_count
-            ).astype(BF16)
-    gate_t = (wg_ref[...].astype(F32) * 0.5).astype(BF16).T
-    up_t = wu_ref[...].T
+    tall = jnp.broadcast_to(
+        right.astype(BF16).astype(F32)[:, None, :], (outer, GROUP, col_count)
+    ).reshape(outer * GROUP, col_count)
+    sub = lax.rem(lax.broadcasted_iota(jnp.int32, tall.shape, 0), GROUP)
+    for r in range(GROUP):
+        blocks_scr[:, r * col_count : (r + 1) * col_count] = jnp.where(sub == r, tall, 0.0).astype(
+            BF16
+        )
+    eye_scr[...] = (
+        lax.broadcasted_iota(jnp.int32, eye_scr.shape, 0)
+        == lax.broadcasted_iota(jnp.int32, eye_scr.shape, 1)
+    ).astype(BF16)
+    gate_t = (wg_ref[...].T.astype(F32) * (pgain_ref[...] * 0.5)).astype(BF16)
+    up_t = (wu_ref[...].T.astype(F32) * pgain_ref[...]).astype(BF16)
     for m in range(hid // 16):
         wgu_scr[32 * m : 32 * m + 16, :] = gate_t[16 * m : 16 * m + 16]
         wgu_scr[32 * m + 16 : 32 * m + 32, :] = up_t[16 * m : 16 * m + 16]
@@ -239,7 +242,6 @@
     high = scaled.astype(BF16)
     wb_scr[:head_count] = high
     wb_scr[head_count:] = (scaled - high.astype(F32)).astype(BF16)
-    gain_scr[...] = jnp.broadcast_to(pgain_ref[...], (col_count, pair_width)).T
     keys = col_start + lax.broadcasted_iota(jnp.int32, (8, col_count), 1)
     live_scr[...] = (keys < limit).astype(F32)
     wo_scr[...] = wo_ref[...].astype(F32)
@@ -249,8 +251,11 @@
         w0 = wo_scr[pl.ds(d, outer, stride=outer), :]
         w1 = wo_scr[pl.ds(d + 1, outer, stride=outer), :]
         both = matmul(left, jnp.concatenate([w0, w1], axis=1).astype(BF16))
-        t_scr[d] = both[:, :pair_width]
-        t_scr[d + 1] = both[:, pair_width:]
+        split = (group_total, GROUP, pair_width)
+        both = jnp.concatenate(
+            [both[:, :pair_width].reshape(split), both[:, pair_width:].reshape(split)], axis=1
+        )
+        t_scr[:, pl.ds(pl.multiple_of(pair * 2 * GROUP, 8), 2 * GROUP), :] = both
         return carry
 
     lax.fori_loop(0, outer // 2, table, 0)
@@ -306,58 +311,64 @@
                 lax.rsqrt(variance + EPSILON), (8, col_count)
             )
 
-    def expand(index, count, part):
-        size = hid // count
-        both = matmul(wgu_scr[2 * index * size : 2 * (index + 1) * size], normed_scr[part])
-        base = index * size
+    def expand(quarter, part):
+        size = hid // 4
+        both = matmul(wgu_scr[2 * quarter * size : 2 * (quarter + 1) * size], normed_scr[part])
+        base = quarter * size
         for m in range(size // 16):
             half_gate, up = both[32 * m : 32 * m + 16], both[32 * m + 16 : 32 * m + 32]
             hidden = (half_gate * jnp.tanh(half_gate) + half_gate) * up
             hidden_scr[part, base + 16 * m : base + 16 * m + 16, :] = hidden.astype(BF16)
 
     def update(group, part):
-        rows = pl.ds(pl.multiple_of(group // (8 // GROUP) * 8, 8), 8)
-        table_t = t_scr[:, rows, :].reshape(outer * 8, pair_width).astype(BF16).T
-        added = matmul(table_t, blocks_scr[lax.rem(group, 8 // GROUP)])
+        table_t = jnp.concatenate([t_scr[group].astype(BF16).T, eye_scr[...]], axis=1)
+        pair_t = [pair_scr[group * GROUP + r].T for r in range(GROUP)]
+        total = jnp.concatenate([blocks_scr[...], jnp.concatenate(pair_t, axis=1)], axis=0)
+        added = matmul(table_t, total)
         for r in range(GROUP):
-            middle = pair_scr[group * GROUP + r].T.astype(F32) + added[:, lanes(r)]
+            middle = added[:, lanes(r)]
             middle_scr[part, :, lanes(r)] = middle
             centered = middle - jnp.mean(middle, axis=0, keepdims=True)
             variance = jnp.mean(centered * centered, axis=0, keepdims=True)
-            normed = centered * lax.rsqrt(variance + EPSILON) * gain_scr[...]
+            normed = centered * lax.rsqrt(variance + EPSILON)
             normed_scr[part, :, lanes(r)] = normed.astype(BF16)
 
-    def clamp(group):
-        return jnp.clip(group, 0, group_total - 1)
-
-    def block(b, carry):
-        @pl.when(b < block_total)
-        def _():
-            block_in(b).wait()
-
+    def block(b, live):
         for u in range(per_block):
             s = b * per_block + u
             part = u % 2
-            owner = jnp.maximum(b - 1, 0) if u < 3 else b
+            owner = b - 1 if u < 3 else b
             at = (u + 1) % per_block
-            weights = score(clamp(s - 3), owner, at, 1 - part)
-            expand(0, 4, 1 - part)
-            project(clamp(s - 2), part)
-            expand(1, 4, 1 - part)
-            update(clamp(s), part)
-            expand(2, 4, 1 - part)
-            collect(owner, at, weights)
-            expand(3, 4, 1 - part)
-
-        @pl.when(b > 0)
-        def _():
-            block_out(b - 1).start()
-
+            if live(u - 3):
+                weights = score(s - 3, owner, at, 1 - part)
+            if live(u - 1):
+                expand(0, 1 - part)
+            if live(u - 2):
+                project(s - 2, part)
+            if live(u - 1):
+                expand(1, 1 - part)
+            if live(u):
+                update(s, part)
+            if live(u - 1):
+                expand(2, 1 - part)
+            if live(u - 3):
+                collect(owner, at, weights)
+            if live(u - 1):
+                expand(3, 1 - part)
+
+    def body(b, carry):
+        block_in(b).wait()
+        block(b, lambda k: True)
+        block_out(b - 1).start()
         return carry
 
-    lax.fori_loop(0, block_total + 1, block, 0)
-    num_ref[...] = num_scr[:block_total].astype(BF16)
-    stat_ref[...] = stat_scr[:block_total]
+    block_in(0).wait()
+    block(0, lambda k: k >= 0)
+    lax.fori_loop(1, block_total, body, 0)
+    block(block_total, lambda k: k < 0)
+    block_out(block_total - 1).start()
+    num_ref[...] = num_scr[...].astype(BF16)
+    stat_ref[...] = stat_scr[...]
     for b in range(block_total):
         block_out(b).wait()
 
@@ -386,23 +397,23 @@
             pltpu.VMEM(pair_input.shape, BF16),
             pltpu.VMEM(pair_input.shape, BF16),
             pltpu.VMEM((outer * outer, pair_width), F32),
-            pltpu.VMEM((outer, row_count, pair_width), F32),
-            pltpu.VMEM((8 // GROUP, outer * 8, tokens), BF16),
+            pltpu.VMEM((row_count // GROUP, outer * GROUP, pair_width), F32),
+            pltpu.VMEM((outer * GROUP, tokens), BF16),
             pltpu.VMEM((row_count // GROUP, GROUP, width), F32),
             pltpu.VMEM((width, col_count), BF16),
             pltpu.VMEM((col_count, width), BF16),
             pltpu.VMEM((2 * hid, pair_width), BF16),
             pltpu.VMEM((pair_width, hid), BF16),
             pltpu.VMEM((2 * head_count, pair_width), BF16),
-            pltpu.VMEM((pair_width, col_count), F32),
+            pltpu.VMEM((pair_width, pair_width), BF16),
             pltpu.VMEM((8, col_count), F32),
             pltpu.VMEM((2, pair_width, tokens), BF16),
             pltpu.VMEM((2, pair_width, tokens), F32),
             pltpu.VMEM((2, hid, tokens), BF16),
             pltpu.VMEM((2, pair_width, tokens), BF16),
             pltpu.VMEM((2, 8, tokens), F32),
-            pltpu.VMEM((row_count // BLOCK + 1, BLOCK // GROUP, GROUP * width), F32),
-            pltpu.VMEM((row_count // BLOCK + 1, BLOCK // GROUP, 128), F32),
+            pltpu.VMEM((row_count // BLOCK, BLOCK // GROUP, GROUP * width), F32),
+            pltpu.VMEM((row_count // BLOCK, BLOCK // GROUP, 128), F32),
             pltpu.SemaphoreType.DMA((row_count // BLOCK,)),
             pltpu.SemaphoreType.DMA((row_count // BLOCK,)),
         ],

time: 78.4 us -> 74.9 us (0.955)
  Pallas kernels: 76.2 us -> 72.7 us
    pallas_call x1, Pallas kernels: 45.3 us -> 41.8 us  [main(): pl.pallas_call(functools.partial(main_kernel, head_count, row_devices), o...]
where the time goes in v4:
time: 74.9 us; the launch traced here: 74.7 us
  Pallas kernels  72.7 us (97%)
  local copies, waits for them, and re-layouts  1.31 us (2%)
    pallas_call x1, Pallas kernels, main(): pl.pallas_call(functools.partial(main_kernel, head_count, row_devices), o...  41.8 us
    pallas_call x1, Pallas kernels, gather(): pl.pallas_call(functools.partial(gather_kernel, rows, cols, per_block), o...  18.1 us
    pallas_call x1, Pallas kernels, combine(): pl.pallas_call(functools.partial(combine_kernel, cols, head_count), out_s...  12.8 us

profile of v4, /device:TPU:1, one launch (start us, length us, event | category | flops | bytes accessed | tf_op | source)
XLA Modules:
  0.0 74.7 jit_solution(9108017364777462351)
XLA Ops:
  0.6 18.1 %gather_tokens.1 = (bf16[256,384]{1,0:T(8,128)(2,1)}, bf16[128,384]{1,0:T(8,128)(2,1)}) custom-call(bf16[16,384]{1,0:T(8,128)(2,1)} %single_ref.3), custom_call_target="tpu_custom_call" | custom-call | tf_op jit(solution)/shard_map/gather_tokens/pallas_call | solution.py:124
  18.8 41.8 %pair_main.1 = (bf16[256,128,128]{2,1,0:T(8,128)(2,1)}, bf16[16,4,1536]{2,1,0:T(4,128)(2,1)}, f32[16,4,128]{2,1,0:T(4,128)}) custom-call(s32[8]{0:T(128)} %seg_ref.1, bf16[256,384]{1,0:T(8,128)(2,1)} %get-tuple-element.7.row_ref, bf16[128,384]{1,0:T(8,128)(2,1)} %get-tuple-element.8.col_ref, f32[384]{0:T(512)} %sgain_ref.3, bf16[32,384]{1,0:T(8,128)(2,1)} %bitcast.5, ...), custom_call_target="tpu_custom_call" | custom-call | tf_op jit(solution)/shard_map/pair_main/pallas_call | solution.py:383
  60.6 12.8 %combine_parts.1 = bf16[16,384]{1,0:T(8,128)(2,1)} custom-call(bf16[16,384]{1,0:T(8,128)(2,1)} %single_ref.3, f32[384]{0:T(512)} %sgain_ref.3, bf16[384,384]{1,0:T(8,128)(2,1)} %wga_ref.1, bf16[384,384]{1,0:T(8,128)(2,1)} %wo_ref.3, bf16[16,4,1536]{2,1,0:T(4,128)(2,1)} %get-tuple-element.9.num_ref, f32[16,4,128]{2,1,0:T(4,128)} %get-tuple-element.10.stat_ref), custom_call_target="tpu_custom_call" | custom-call | tf_op jit(solution)/shard_map/combine_parts/pallas_call | solution.py:523
  73.4 1.3 %copy.21 = bf16[16,384]{1,0:T(8,128)(2,1)} copy(bf16[16,384]{1,0:T(8,128)(2,1)} %combine_parts.1) | data formatting | bytes 24576

commit v5 on v4

--- a/solution.py
+++ b/solution.py
@@ -13,6 +13,7 @@
 BF16 = jnp.bfloat16
 F32 = jnp.float32
 VMEM_SPEC = pl.BlockSpec(memory_space=pltpu.VMEM)
+ANY_SPEC = pl.BlockSpec(memory_space=pl.ANY)
 GROUP = 4
 BLOCK = 16
 
@@ -35,9 +36,25 @@
 
 
 def gather_kernel(
-    rows, cols, per_block, single_ref, row_ref, col_ref, send_row, send_col, recv_row, recv_col
+    rows,
+    cols,
+    per_block,
+    single_ref,
+    wo_ref,
+    row_ref,
+    col_ref,
+    wt_ref,
+    wo_scr,
+    wide_scr,
+    wt_scr,
+    send_row,
+    send_col,
+    recv_row,
+    recv_col,
+    outer_sems,
 ):
     own = single_ref.shape[0]
+    outer, pair_width = wt_scr.shape[0], wo_scr.shape[1]
     row, col = lax.axis_index("row"), lax.axis_index("col")
     linear = row * cols + col
     target_col = linear // per_block
@@ -60,6 +77,9 @@
                 barrier, inc=1, device_id=(source_row, source_col), device_id_type=MESH
             )
 
+    outer_in = pltpu.make_async_copy(wo_ref, wo_scr, outer_sems.at[0])
+    outer_out = pltpu.make_async_copy(wt_scr, wt_ref, outer_sems.at[1])
+    outer_in.start()
     pl.semaphore_wait(barrier, cols - 1 + rows - is_own.astype(jnp.int32))
 
     own_rows = pl.ds(pl.multiple_of(col * own, own), own)
@@ -101,6 +121,13 @@
     @pl.when(is_own)
     def _():
         local_col.start()
+
+    outer_in.wait()
+    wide_scr[...] = wo_scr[...].astype(F32)
+    for d in range(outer):
+        rows_d = wide_scr[pl.ds(d, outer, stride=outer), :]
+        wt_scr[:, d * pair_width : (d + 1) * pair_width] = rows_d.astype(BF16)
+    outer_out.start()
 
     for sender in range(cols):
         block = row_ref.at[pl.ds(sender * own, own)]
@@ -117,27 +144,35 @@
     def _():
         col_copy(0).wait_send()
 
-
-def gather(single, rows, cols, row_count, col_count):
+    outer_out.wait()
+
+
+def gather(single, w_outer, outer, rows, cols, row_count, col_count):
     own, width = single.shape
+    lanes = w_outer.shape[0] // outer * w_outer.shape[1]
     per_block = col_count // own
     return pl.pallas_call(
         functools.partial(gather_kernel, rows, cols, per_block),
         out_shape=(
             jax.ShapeDtypeStruct((row_count, width), single.dtype),
             jax.ShapeDtypeStruct((col_count, width), single.dtype),
+            jax.ShapeDtypeStruct((outer, lanes), BF16),
         ),
-        in_specs=[VMEM_SPEC],
-        out_specs=(VMEM_SPEC, VMEM_SPEC),
+        in_specs=[ANY_SPEC] * 2,
+        out_specs=(ANY_SPEC,) * 3,
         scratch_shapes=[
+            pltpu.VMEM(w_outer.shape, BF16),
+            pltpu.VMEM(w_outer.shape, F32),
+            pltpu.VMEM((outer, lanes), BF16),
             pltpu.SemaphoreType.DMA((cols,)),
             pltpu.SemaphoreType.DMA((rows,)),
             pltpu.SemaphoreType.DMA((cols,)),
             pltpu.SemaphoreType.DMA((per_block,)),
+            pltpu.SemaphoreType.DMA((2,)),
         ],
         compiler_params=pltpu.CompilerParams(collective_id=0, has_side_effects=True),
         name="gather_tokens",
-    )(single)
+    )(single, w_outer)
 
 
 def main_kernel(
@@ -165,7 +200,6 @@
     stat_ref,
     pair_scr,
     out_scr,
-    wo_scr,
     t_scr,
     blocks_scr,
     q_scr,
@@ -244,21 +278,13 @@
     wb_scr[head_count:] = (scaled - high.astype(F32)).astype(BF16)
     keys = col_start + lax.broadcasted_iota(jnp.int32, (8, col_count), 1)
     live_scr[...] = (keys < limit).astype(F32)
-    wo_scr[...] = wo_ref[...].astype(F32)
-
-    def table(pair, carry):
-        d = pair * 2
-        w0 = wo_scr[pl.ds(d, outer, stride=outer), :]
-        w1 = wo_scr[pl.ds(d + 1, outer, stride=outer), :]
-        both = matmul(left, jnp.concatenate([w0, w1], axis=1).astype(BF16))
+    for pair in range(outer // 2):
+        both = matmul(left, wo_ref[:, pair * 2 * pair_width : (pair + 1) * 2 * pair_width])
         split = (group_total, GROUP, pair_width)
         both = jnp.concatenate(
             [both[:, :pair_width].reshape(split), both[:, pair_width:].reshape(split)], axis=1
         )
-        t_scr[:, pl.ds(pl.multiple_of(pair * 2 * GROUP, 8), 2 * GROUP), :] = both
-        return carry
-
-    lax.fori_loop(0, outer // 2, table, 0)
+        t_scr[:, pair * 2 * GROUP : (pair + 1) * 2 * GROUP, :] = both
 
     own_head = (
         lax.broadcasted_iota(jnp.int32, (GROUP, head_count, width), 2) // head_dim
@@ -379,7 +405,6 @@
     outer = weights[1].shape[0]
     hid = weights[5].shape[1]
     tokens = GROUP * col_count
-    any_spec = pl.BlockSpec(memory_space=pl.ANY)
     return pl.pallas_call(
         functools.partial(main_kernel, head_count, row_devices),
         out_shape=(
@@ -390,13 +415,12 @@
         in_specs=[
             pl.BlockSpec(memory_space=pltpu.SMEM),
             *([VMEM_SPEC] * (2 + len(weights))),
-            any_spec,
+            ANY_SPEC,
         ],
-        out_specs=(any_spec, VMEM_SPEC, VMEM_SPEC),
+        out_specs=(ANY_SPEC, VMEM_SPEC, VMEM_SPEC),
         scratch_shapes=[
             pltpu.VMEM(pair_input.shape, BF16),
             pltpu.VMEM(pair_input.shape, BF16),
-            pltpu.VMEM((outer * outer, pair_width), F32),
             pltpu.VMEM((row_count // GROUP, outer * GROUP, pair_width), F32),
             pltpu.VMEM((outer * GROUP, tokens), BF16),
             pltpu.VMEM((row_count // GROUP, GROUP, width), F32),
@@ -432,10 +456,15 @@
     num_ref,
     stat_ref,
     out_ref,
+    single_scr,
+    sgain_scr,
+    wga_scr,
+    wo_scr,
     nums,
     stats,
     spread_scr,
     attended_scr,
+    load_sems,
     send_num,
     send_stat,
     recv_num,
@@ -451,8 +480,23 @@
         pl.semaphore_signal(
             barrier, inc=1, device_id=(row, lax.rem(col + step, cols)), device_id_type=MESH
         )
-    single = single_ref[...].astype(F32)
-    gate = matmul(normalize(single, sgain_ref[...]).astype(BF16), wga_ref[...])
+    loads = [
+        pltpu.make_async_copy(source, target, load_sems.at[i])
+        for i, (source, target) in enumerate(
+            (
+                (single_ref, single_scr),
+                (sgain_ref, sgain_scr),
+                (wga_ref, wga_scr),
+                (wo_ref, wo_scr),
+            )
+        )
+    ]
+    for load in loads:
+        load.start()
+    for load in loads:
+        load.wait()
+    single = single_scr[...].astype(F32)
+    gate = matmul(normalize(single, sgain_scr[...]).astype(BF16), wga_scr[...])
     gate = jax.nn.sigmoid(gate)
     lane = lax.rem(lax.broadcasted_iota(jnp.int32, (256, width), 0), 128)
     head = lax.broadcasted_iota(jnp.int32, (256, width), 1) // head_dim
@@ -512,7 +556,7 @@
                 g : g + 1, r * width : (r + 1) * width
             ]
     gated = (gate * attended_scr[...]).astype(BF16)
-    out_ref[...] = (single + matmul(gated, wo_ref[...])).astype(BF16)
+    out_ref[...] = (single + matmul(gated, wo_scr[...])).astype(BF16)
     for step in range(1, cols):
         for copy in copies(step):
             copy.wait_send()
@@ -523,13 +567,18 @@
     return pl.pallas_call(
         functools.partial(combine_kernel, cols, head_count),
         out_shape=jax.ShapeDtypeStruct(single.shape, BF16),
-        in_specs=[VMEM_SPEC] * 6,
+        in_specs=[ANY_SPEC] * 6,
         out_specs=VMEM_SPEC,
         scratch_shapes=[
+            pltpu.VMEM(single.shape, BF16),
+            pltpu.VMEM(single_gain.shape, F32),
+            pltpu.VMEM(w_gate_attn.shape, BF16),
+            pltpu.VMEM(w_output.shape, BF16),
             pltpu.VMEM((cols, *num.shape[1:]), BF16),
             pltpu.VMEM((cols, *stat.shape[1:]), F32),
             pltpu.VMEM((256, GROUP * width), BF16),
             pltpu.VMEM((own, width), F32),
+            pltpu.SemaphoreType.DMA((4,)),
             pltpu.SemaphoreType.DMA((cols,)),
             pltpu.SemaphoreType.DMA((cols,)),
             pltpu.SemaphoreType.DMA((cols,)),
@@ -564,12 +613,14 @@
 ):
     row_count, col_count, _ = pair_input.shape
     head_count = w_bias.shape[1]
-    row_tokens, col_tokens = gather(single, rows, cols, row_count, col_count)
+    row_tokens, col_tokens, outer_table = gather(
+        single, w_outer, w_left.shape[1], rows, cols, row_count, col_count
+    )
     weights = (
         single_gain,
         w_left.T,
         w_right.T,
-        w_outer,
+        outer_table,
         pair_gain[None, :],
         w_gate,
         w_up,

time: 74.9 us -> 70.7 us (0.944)
  Pallas kernels: 72.7 us -> 68.5 us
    pallas_call x1, Pallas kernels: 41.8 us -> 39.2 us  [main(): pl.pallas_call(functools.partial(main_kernel, head_count, row_devices), o...]
    pallas_call x1, Pallas kernels: 18.1 us -> 17.3 us  [gather(): pl.pallas_call(functools.partial(gather_kernel, rows, cols, per_block), o...]
where the time goes in v5:
time: 70.7 us; the launch traced here: 70.5 us
  Pallas kernels  68.5 us (97%)
  local copies, waits for them, and re-layouts  1.31 us (2%)
    pallas_call x1, Pallas kernels, main(): pl.pallas_call(functools.partial(main_kernel, head_count, row_devices), o...  39.2 us
    pallas_call x1, Pallas kernels, gather(): pl.pallas_call(functools.partial(gather_kernel, rows, cols, per_block), o...  17.3 us
    pallas_call x1, Pallas kernels, combine(): pl.pallas_call(functools.partial(combine_kernel, cols, head_count), out_s...  12 us

profile of v5, /device:TPU:1, one launch (start us, length us, event | category | flops | bytes accessed | tf_op | source)
XLA Modules:
  0.0 70.5 jit_solution(10666612307250756665)
XLA Ops:
  0.6 17.3 %gather_tokens.1 = (bf16[256,384]{1,0:T(8,128)(2,1)}, bf16[128,384]{1,0:T(8,128)(2,1)}, bf16[32,4096]{1,0:T(8,128)(2,1)}) custom-call(bf16[16,384]{1,0:T(8,128)(2,1)} %single_ref.3, bf16[1024,128]{1,0:T(8,128)(2,1)} %wo_ref.2), custom_call_target="tpu_custom_call" | custom-call | tf_op jit(solution)/shard_map/gather_tokens/pallas_call | solution.py:154
  17.9 39.2 %pair_main.1 = (bf16[256,128,128]{2,1,0:T(8,128)(2,1)}, bf16[16,4,1536]{2,1,0:T(4,128)(2,1)}, f32[16,4,128]{2,1,0:T(4,128)}) custom-call(s32[8]{0:T(128)} %seg_ref.1, bf16[256,384]{1,0:T(8,128)(2,1)} %get-tuple-element.8.row_ref, bf16[128,384]{1,0:T(8,128)(2,1)} %get-tuple-element.9.col_ref, f32[384]{0:T(512)} %sgain_ref.3, bf16[32,384]{1,0:T(8,128)(2,1)} %bitcast.5, ...), custom_call_target="tpu_custom_call" | custom-call | tf_op jit(solution)/shard_map/pair_main/pallas_call | solution.py:408
  57.1 12.0 %combine_parts.1 = bf16[16,384]{1,0:T(8,128)(2,1)} custom-call(bf16[16,384]{1,0:T(8,128)(2,1)} %single_ref.3, f32[384]{0:T(512)} %sgain_ref.3, bf16[384,384]{1,0:T(8,128)(2,1)} %wga_ref.1, bf16[384,384]{1,0:T(8,128)(2,1)} %wo_ref.3, bf16[16,4,1536]{2,1,0:T(4,128)(2,1)} %get-tuple-element.11.num_ref, f32[16,4,128]{2,1,0:T(4,128)} %get-tuple-element.12.stat_ref), custom_call_target="tpu_custom_call" | custom-call | tf_op jit(solution)/shard_map/combine_parts/pallas_call | solution.py:567
  69.2 1.3 %copy.21 = bf16[16,384]{1,0:T(8,128)(2,1)} copy(bf16[16,384]{1,0:T(8,128)(2,1)} %combine_parts.1) | data formatting | bytes 24576

commit v6 on v5

--- a/solution.py
+++ b/solution.py
@@ -14,6 +14,11 @@
 F32 = jnp.float32
 VMEM_SPEC = pl.BlockSpec(memory_space=pltpu.VMEM)
 ANY_SPEC = pl.BlockSpec(memory_space=pl.ANY)
+
+
+def in_vmem(array):
+    return pltpu.with_memory_space_constraint(array, pltpu.VMEM)
+
 GROUP = 4
 BLOCK = 16
 
@@ -35,26 +40,13 @@
     )
 
 
-def gather_kernel(
-    rows,
-    cols,
-    per_block,
-    single_ref,
-    wo_ref,
-    row_ref,
-    col_ref,
-    wt_ref,
-    wo_scr,
-    wide_scr,
-    wt_scr,
-    send_row,
-    send_col,
-    recv_row,
-    recv_col,
-    outer_sems,
-):
+def gather_kernel(rows, cols, per_block, weight_count, *refs):
+    single_ref, wo_ref, *weights = refs[: 2 + weight_count]
+    row_ref, col_ref, wt_ref, *copied = refs[2 + weight_count : 5 + 2 * weight_count]
+    scratch = refs[5 + 2 * weight_count :]
+    wo_scr, wide_scr, send_row, send_col, recv_row, recv_col, outer_sem, weight_sems = scratch
     own = single_ref.shape[0]
-    outer, pair_width = wt_scr.shape[0], wo_scr.shape[1]
+    outer, pair_width = wt_ref.shape[0], wo_scr.shape[1]
     row, col = lax.axis_index("row"), lax.axis_index("col")
     linear = row * cols + col
     target_col = linear // per_block
@@ -77,9 +69,14 @@
                 barrier, inc=1, device_id=(source_row, source_col), device_id_type=MESH
             )
 
-    outer_in = pltpu.make_async_copy(wo_ref, wo_scr, outer_sems.at[0])
-    outer_out = pltpu.make_async_copy(wt_scr, wt_ref, outer_sems.at[1])
+    outer_in = pltpu.make_async_copy(wo_ref, wo_scr, outer_sem)
     outer_in.start()
+    loads = [
+        pltpu.make_async_copy(source, target, weight_sems.at[i])
+        for i, (source, target) in enumerate(zip(weights, copied))
+    ]
+    for load in loads:
+        load.start()
     pl.semaphore_wait(barrier, cols - 1 + rows - is_own.astype(jnp.int32))
 
     own_rows = pl.ds(pl.multiple_of(col * own, own), own)
@@ -126,8 +123,7 @@
     wide_scr[...] = wo_scr[...].astype(F32)
     for d in range(outer):
         rows_d = wide_scr[pl.ds(d, outer, stride=outer), :]
-        wt_scr[:, d * pair_width : (d + 1) * pair_width] = rows_d.astype(BF16)
-    outer_out.start()
+        wt_ref[:, d * pair_width : (d + 1) * pair_width] = rows_d.astype(BF16)
 
     for sender in range(cols):
         block = row_ref.at[pl.ds(sender * own, own)]
@@ -144,35 +140,37 @@
     def _():
         col_copy(0).wait_send()
 
-    outer_out.wait()
-
-
-def gather(single, w_outer, outer, rows, cols, row_count, col_count):
+    for load in loads:
+        load.wait()
+
+
+def gather(single, w_outer, weights, outer, rows, cols, row_count, col_count):
     own, width = single.shape
     lanes = w_outer.shape[0] // outer * w_outer.shape[1]
     per_block = col_count // own
     return pl.pallas_call(
-        functools.partial(gather_kernel, rows, cols, per_block),
+        functools.partial(gather_kernel, rows, cols, per_block, len(weights)),
         out_shape=(
-            jax.ShapeDtypeStruct((row_count, width), single.dtype),
-            jax.ShapeDtypeStruct((col_count, width), single.dtype),
-            jax.ShapeDtypeStruct((outer, lanes), BF16),
+            pltpu.VMEM((row_count, width), single.dtype),
+            pltpu.VMEM((col_count, width), single.dtype),
+            pltpu.VMEM((outer, lanes), BF16),
+            *[pltpu.VMEM(w.shape, w.dtype) for w in weights],
         ),
-        in_specs=[ANY_SPEC] * 2,
-        out_specs=(ANY_SPEC,) * 3,
+        in_specs=[ANY_SPEC] * (2 + len(weights)),
+        out_specs=(VMEM_SPEC,) * (3 + len(weights)),
         scratch_shapes=[
             pltpu.VMEM(w_outer.shape, BF16),
             pltpu.VMEM(w_outer.shape, F32),
-            pltpu.VMEM((outer, lanes), BF16),
             pltpu.SemaphoreType.DMA((cols,)),
             pltpu.SemaphoreType.DMA((rows,)),
             pltpu.SemaphoreType.DMA((cols,)),
             pltpu.SemaphoreType.DMA((per_block,)),
-            pltpu.SemaphoreType.DMA((2,)),
+            pltpu.SemaphoreType.DMA,
+            pltpu.SemaphoreType.DMA((len(weights),)),
         ],
         compiler_params=pltpu.CompilerParams(collective_id=0, has_side_effects=True),
         name="gather_tokens",
-    )(single, w_outer)
+    )(single, w_outer, *weights)
 
 
 def main_kernel(
@@ -441,9 +439,9 @@
             pltpu.SemaphoreType.DMA((row_count // BLOCK,)),
             pltpu.SemaphoreType.DMA((row_count // BLOCK,)),
         ],
-        compiler_params=pltpu.CompilerParams(vmem_limit_bytes=56 << 20),
+        compiler_params=pltpu.CompilerParams(vmem_limit_bytes=54 << 20),
         name="pair_main",
-    )(seg, row_tokens, col_tokens, *weights, pair_input)
+    )(seg, *[in_vmem(x) for x in (row_tokens, col_tokens, *weights)], pair_input)
 
 
 def combine_kernel(
@@ -566,7 +564,7 @@
     own, width = single.shape
     return pl.pallas_call(
         functools.partial(combine_kernel, cols, head_count),
-        out_shape=jax.ShapeDtypeStruct(single.shape, BF16),
+        out_shape=pltpu.VMEM(single.shape, BF16),
         in_specs=[ANY_SPEC] * 6,
         out_specs=VMEM_SPEC,
         scratch_shapes=[
@@ -613,24 +611,30 @@
 ):
     row_count, col_count, _ = pair_input.shape
     head_count = w_bias.shape[1]
-    row_tokens, col_tokens, outer_table = gather(
-        single, w_outer, w_left.shape[1], rows, cols, row_count, col_count
+    row_tokens, col_tokens, outer_table, *weights = gather(
+        single,
+        w_outer,
+        (
+            single_gain,
+            w_left.T,
+            w_right.T,
+            pair_gain[None, :],
+            w_gate,
+            w_up,
+            w_down,
+            bias_gain[None, :],
+            w_bias.T,
+            w_query,
+            w_key,
+            w_value,
+        ),
+        w_left.shape[1],
+        rows,
+        cols,
+        row_count,
+        col_count,
     )
-    weights = (
-        single_gain,
-        w_left.T,
-        w_right.T,
-        outer_table,
-        pair_gain[None, :],
-        w_gate,
-        w_up,
-        w_down,
-        bias_gain[None, :],
-        w_bias.T,
-        w_query,
-        w_key,
-        w_value,
-    )
+    weights = (*weights[:3], outer_table, *weights[3:])
     pair_out, num, stat = main(
         head_count, rows, segment_lengths, row_tokens, col_tokens, weights, pair_input
     )

time: 70.7 us -> 69.6 us (0.984)
  local copies, waits for them, and re-layouts: 1.31 us -> 0.6 us
where the time goes in v6:
time: 69.6 us; the launch traced here: 69.3 us
  Pallas kernels  68.1 us (98%)
    pallas_call x1, Pallas kernels, main(): pl.pallas_call(functools.partial(main_kernel, head_count, row_devices), o...  39.4 us
    pallas_call x1, Pallas kernels, gather(): pl.pallas_call(functools.partial(gather_kernel, rows, cols, per_block, le...  17.3 us
    pallas_call x1, Pallas kernels, combine(): pl.pallas_call(functools.partial(combine_kernel, cols, head_count), out_s...  11.4 us

profile of v6, /device:TPU:1, one launch (start us, length us, event | category | flops | bytes accessed | tf_op | source)
XLA Modules:
  0.0 69.3 jit_solution(5620010479119834208)
XLA Ops:
  0.6 17.3 %gather_tokens.1 = (bf16[256,384]{1,0:T(8,128)(2,1)S(1)}, bf16[128,384]{1,0:T(8,128)(2,1)S(1)}, bf16[32,4096]{1,0:T(8,128)(2,1)S(1)}, f32[384]{0:T(512)S(1)}, bf...) custom-call(bf16[16,384]{1,0:T(8,128)(2,1)} %single_ref.1, ...), custom_call_target="tpu_custom_call" | custom-call | tf_op jit(solution)/shard_map/gather_tokens/pallas_call | solution.py:151
  17.9 39.4 %pair_main.1 = (bf16[256,128,128]{2,1,0:T(8,128)(2,1)}, bf16[16,4,1536]{2,1,0:T(4,128)(2,1)}, f32[16,4,128]{2,1,0:T(4,128)}) custom-call(s32[8]{0:T(128)} %seg_ref.1, bf16[256,384]{1,0:T(8,128)(2,1)S(1)} %get-tuple-element.20.row_ref, bf16[128,384]{1,0:T(8,128)(2,1)S(1)} %get-tuple-element.21.col_ref, f32[384]{0:T(512)S(1)} %get-tuple-element.22.sgain_ref, ...), custom_call_target="tpu_custom_call" | custom-call | tf_op jit(solution)/shard_map/pair_main/pallas_call | solution.py:406
  57.3 11.4 %combine_parts.1 = bf16[16,384]{1,0:T(8,128)(2,1)S(1)} custom-call(bf16[16,384]{1,0:T(8,128)(2,1)} %single_ref.1, f32[384]{0:T(512)} %sgain_ref.1, bf16[384,384]{1,0:T(8,128)(2,1)} %wga_ref.1, bf16[384,384]{1,0:T(8,128)(2,1)} %wo_ref.1, bf16[16,4,1536]{2,1,0:T(4,128)(2,1)} %get-tuple-element.35.num_ref, f32[16,4,128]{2,1,0:T(4,128)} %get-tuple-element.36.stat_ref), custom_call_target="tpu_custom_call" | custom-call | tf_op jit(solution)/shard_map/combine_parts/pallas_call | solution.py:565
  68.7 0.6 copy.21

commit v7 on v6

--- a/solution.py
+++ b/solution.py
@@ -407,8 +407,8 @@
         functools.partial(main_kernel, head_count, row_devices),
         out_shape=(
             jax.ShapeDtypeStruct(pair_input.shape, BF16),
-            jax.ShapeDtypeStruct((row_count // BLOCK, BLOCK // GROUP, GROUP * width), BF16),
-            jax.ShapeDtypeStruct((row_count // BLOCK, BLOCK // GROUP, 128), F32),
+            pltpu.VMEM((row_count // BLOCK, BLOCK // GROUP, GROUP * width), BF16),
+            pltpu.VMEM((row_count // BLOCK, BLOCK // GROUP, 128), F32),
         ),
         in_specs=[
             pl.BlockSpec(memory_space=pltpu.SMEM),
@@ -565,7 +565,7 @@
     return pl.pallas_call(
         functools.partial(combine_kernel, cols, head_count),
         out_shape=pltpu.VMEM(single.shape, BF16),
-        in_specs=[ANY_SPEC] * 6,
+        in_specs=[ANY_SPEC] * 4 + [VMEM_SPEC] * 2,
         out_specs=VMEM_SPEC,
         scratch_shapes=[
             pltpu.VMEM(single.shape, BF16),
@@ -582,9 +582,11 @@
             pltpu.SemaphoreType.DMA((cols,)),
             pltpu.SemaphoreType.DMA((cols,)),
         ],
-        compiler_params=pltpu.CompilerParams(collective_id=1, has_side_effects=True),
+        compiler_params=pltpu.CompilerParams(
+            collective_id=1, has_side_effects=True, vmem_limit_bytes=54 << 20
+        ),
         name="combine_parts",
-    )(single, single_gain, w_gate_attn, w_output, num, stat)
+    )(single, single_gain, w_gate_attn, w_output, in_vmem(num), in_vmem(stat))
 
 
 def on_device(

time: 69.6 us -> 68.7 us (0.987)
  Pallas kernels: 68.1 us -> 67.2 us
where the time goes in v7:
time: 68.7 us; the launch traced here: 68.4 us
  Pallas kernels  67.2 us (98%)
    pallas_call x1, Pallas kernels, main(): pl.pallas_call(functools.partial(main_kernel, head_count, row_devices), o...  38.7 us
    pallas_call x1, Pallas kernels, gather(): pl.pallas_call(functools.partial(gather_kernel, rows, cols, per_block, le...  17.3 us
    pallas_call x1, Pallas kernels, combine(): pl.pallas_call(functools.partial(combine_kernel, cols, head_count), out_s...  11.2 us

profile of v7, /device:TPU:1, one launch (start us, length us, event | category | flops | bytes accessed | tf_op | source)
XLA Modules:
  0.0 68.4 jit_solution(5140812985157590687)
XLA Ops:
  0.6 17.3 %gather_tokens.1 = (bf16[256,384]{1,0:T(8,128)(2,1)S(1)}, bf16[128,384]{1,0:T(8,128)(2,1)S(1)}, bf16[32,4096]{1,0:T(8,128)(2,1)S(1)}, f32[384]{0:T(512)S(1)}, bf...) custom-call(bf16[16,384]{1,0:T(8,128)(2,1)} %single_ref.1, ...), custom_call_target="tpu_custom_call" | custom-call | tf_op jit(solution)/shard_map/gather_tokens/pallas_call | solution.py:151
  17.9 38.7 %pair_main.1 = (bf16[256,128,128]{2,1,0:T(8,128)(2,1)}, bf16[16,4,1536]{2,1,0:T(4,128)(2,1)S(1)}, f32[16,4,128]{2,1,0:T(4,128)S(1)}) custom-call(s32[8]{0:T(128)} %seg_ref.1, bf16[256,384]{1,0:T(8,128)(2,1)S(1)} %get-tuple-element.20.row_ref, bf16[128,384]{1,0:T(8,128)(2,1)S(1)} %get-tuple-element.21.col_ref, f32[384]{0:T(512)S(1)} %get-tuple-element.22.sgain_ref, ...), custom_call_target="tpu_custom_call" | custom-call | tf_op jit(solution)/shard_map/pair_main/pallas_call | solution.py:406
  56.6 11.2 %combine_parts.1 = bf16[16,384]{1,0:T(8,128)(2,1)S(1)} custom-call(bf16[16,384]{1,0:T(8,128)(2,1)} %single_ref.1, f32[384]{0:T(512)} %sgain_ref.1, bf16[384,384]{1,0:T(8,128)(2,1)} %wga_ref.1, bf16[384,384]{1,0:T(8,128)(2,1)} %wo_ref.1, bf16[16,4,1536]{2,1,0:T(4,128)(2,1)S(1)} %get-tuple-element.35.num_ref, f32[16,4,128]{2,1,0:T(4,128)S(1)} %get-tuple-element.36.stat_ref), custom_call_target="tpu_custom_call" | custom-call | tf_op jit(solution)/shard_map/combine_parts/pallas_call | solution.py:565
  67.8 0.6 copy.21

commit v8 on v7

--- a/solution.py
+++ b/solution.py
@@ -55,10 +55,6 @@
     first_source = col * per_block
 
     barrier = pltpu.get_barrier_semaphore()
-    for step in range(1, cols):
-        pl.semaphore_signal(
-            barrier, inc=1, device_id=(row, lax.rem(col + step, cols)), device_id_type=MESH
-        )
     for step in range(per_block):
         source = first_source + step
         source_row, source_col = source // cols, source % cols
@@ -69,6 +65,10 @@
                 barrier, inc=1, device_id=(source_row, source_col), device_id_type=MESH
             )
 
+    for step in range(1, cols):
+        pl.semaphore_signal(
+            barrier, inc=1, device_id=(row, lax.rem(col + step, cols)), device_id_type=MESH
+        )
     outer_in = pltpu.make_async_copy(wo_ref, wo_scr, outer_sem)
     outer_in.start()
     loads = [

time: 68.7 us -> 68.5 us (level)
  no operation moved by 1% of the time
where the time goes in v8:
time: 68.5 us; the launch traced here: 68.3 us
  Pallas kernels  67 us (98%)
    pallas_call x1, Pallas kernels, main(): pl.pallas_call(functools.partial(main_kernel, head_count, row_devices), o...  38.7 us
    pallas_call x1, Pallas kernels, gather(): pl.pallas_call(functools.partial(gather_kernel, rows, cols, per_block, le...  17.1 us
    pallas_call x1, Pallas kernels, combine(): pl.pallas_call(functools.partial(combine_kernel, cols, head_count), out_s...  11.2 us

profile of v8, /device:TPU:1, one launch (start us, length us, event | category | flops | bytes accessed | tf_op | source)
XLA Modules:
  0.0 68.3 jit_solution(14794785125481766909)
XLA Ops:
  0.6 17.1 %gather_tokens.1 = (bf16[256,384]{1,0:T(8,128)(2,1)S(1)}, bf16[128,384]{1,0:T(8,128)(2,1)S(1)}, bf16[32,4096]{1,0:T(8,128)(2,1)S(1)}, f32[384]{0:T(512)S(1)}, bf...) custom-call(bf16[16,384]{1,0:T(8,128)(2,1)} %single_ref.1, ...), custom_call_target="tpu_custom_call" | custom-call | tf_op jit(solution)/shard_map/gather_tokens/pallas_call | solution.py:151
  17.8 38.7 %pair_main.1 = (bf16[256,128,128]{2,1,0:T(8,128)(2,1)}, bf16[16,4,1536]{2,1,0:T(4,128)(2,1)S(1)}, f32[16,4,128]{2,1,0:T(4,128)S(1)}) custom-call(s32[8]{0:T(128)} %seg_ref.1, bf16[256,384]{1,0:T(8,128)(2,1)S(1)} %get-tuple-element.20.row_ref, bf16[128,384]{1,0:T(8,128)(2,1)S(1)} %get-tuple-element.21.col_ref, f32[384]{0:T(512)S(1)} %get-tuple-element.22.sgain_ref, ...), custom_call_target="tpu_custom_call" | custom-call | tf_op jit(solution)/shard_map/pair_main/pallas_call | solution.py:406
  56.5 11.2 %combine_parts.1 = bf16[16,384]{1,0:T(8,128)(2,1)S(1)} custom-call(bf16[16,384]{1,0:T(8,128)(2,1)} %single_ref.1, f32[384]{0:T(512)} %sgain_ref.1, bf16[384,384]{1,0:T(8,128)(2,1)} %wga_ref.1, bf16[384,384]{1,0:T(8,128)(2,1)} %wo_ref.1, bf16[16,4,1536]{2,1,0:T(4,128)(2,1)S(1)} %get-tuple-element.35.num_ref, f32[16,4,128]{2,1,0:T(4,128)S(1)} %get-tuple-element.36.stat_ref), custom_call_target="tpu_custom_call" | custom-call | tf_op jit(solution)/shard_map/combine_parts/pallas_call | solution.py:565
  67.7 0.6 copy.21
